TPU v7x, 32 devices: a whole 2x2x4 slice. The times are simulated.
32 devices in a mesh: shard: 8 (over z, y), rep: 4 (over x, core).
Axes of the slice: x: 2, y: 2, z: 4, core: 2. Of those that a mesh axis runs over, the one named last changes fastest.
Arguments:
- block_input: bfloat16 [4096, 1024], P(('shard', 'rep')), may hold values from -6 to 6
- out_cotangent: bfloat16 [4096, 1024], P(('shard', 'rep')), may hold values from -6 to 6
- w_query: bfloat16 [1024, 1024], P('shard'), may hold values from -0.1875 to 0.1875
- w_key: bfloat16 [1024, 1024], P('shard'), may hold values from -0.1875 to 0.1875
- w_value: bfloat16 [1024, 1024], P('shard'), may hold values from -0.1875 to 0.1875
- w_output: bfloat16 [1024, 1024], P('shard'), may hold values from -0.75 to 0.75
- bias_query: float32 [1024], P('shard'), may hold values from -3 to 3
- bias_value: float32 [1024], P('shard'), may hold values from -3 to 3
- bias_output: float32 [1024], P('shard'), may hold values from -3 to 3
- gain_first: float32 [1024], P('shard'), may hold values from 0.5 to 1.5
- shift_first: float32 [1024], P('shard'), may hold values from -3 to 3
- w_inner: bfloat16 [1024, 4096], P('shard'), may hold values from -0.1875 to 0.1875
- bias_inner: float32 [4096], P('shard'), may hold values from -3 to 3
- w_down: bfloat16 [4096, 1024], P('shard'), may hold values from -0.09375 to 0.09375
- bias_down: float32 [1024], P('shard'), may hold values from -3 to 3
- gain_second: float32 [1024], P('shard'), may hold values from 0.5 to 1.5
- shift_second: float32 [1024], P('shard'), may hold values from -3 to 3
Outputs:
- block_output: bfloat16 [4096, 1024], P(('shard', 'rep'))
- grad_input: bfloat16 [4096, 1024], P(('shard', 'rep'))
- grad_w_query: float32 [1024, 1024], P('shard')
- grad_w_key: float32 [1024, 1024], P('shard')
- grad_w_value: float32 [1024, 1024], P('shard')
- grad_w_output: float32 [1024, 1024], P('shard')
- grad_bias_query: float32 [1024], P('shard')
- grad_bias_value: float32 [1024], P('shard')
- grad_bias_output: float32 [1024], P('shard')
- grad_gain_first: float32 [1024], P('shard')
- grad_shift_first: float32 [1024], P('shard')
- grad_w_inner: float32 [1024, 4096], P('shard')
- grad_bias_inner: float32 [4096], P('shard')
- grad_w_down: float32 [4096, 1024], P('shard')
- grad_bias_down: float32 [1024], P('shard')
- grad_gain_second: float32 [1024], P('shard')
- grad_shift_second: float32 [1024], P('shard')
All inputs are finite; a program needn't handle non-finite values.
Results may differ from a plain program's by a relative error of at most 0.025.
Values may be sent and summed in bfloat16 or wider, within the bound.
A program may use at most 192 MiB of HBM per device.

v0:
```python
import jax
import jax.numpy as jnp
from jax import lax
from jax.sharding import PartitionSpec as P

HEADS = 16
HEAD_DIM = 64
SEQ = 128


EPS = 1e-06
INV_ROOT_TWO = 0.7071067811865476
INV_ROOT_TWO_PI = 0.3989422804014327


def norm_parts(resid):
    centre = resid - jnp.mean(resid, axis=-1, keepdims=True)
    variance = jnp.mean(centre * centre, axis=-1, keepdims=True)
    rstd = lax.rsqrt(variance + EPS)
    return (centre * rstd, rstd)


def norm_back(upstream, normed, rstd):
    return rstd * (
        upstream
        - jnp.mean(upstream, axis=-1, keepdims=True)
        - normed * jnp.mean(upstream * normed, axis=-1, keepdims=True)
    )


def gelu_value(inner):
    return 0.5 * inner * (1.0 + lax.erf(inner * INV_ROOT_TWO))


def gelu_slope(inner):
    return (
        0.5 * (1.0 + lax.erf(inner * INV_ROOT_TWO))
        + inner * jnp.exp(-0.5 * inner * inner) * INV_ROOT_TWO_PI
    )


def score_table(query4, keyed4):
    return jnp.einsum("bqhe,bkhe->bhqk", query4, keyed4) * 0.125


def left_product(left, right):
    return jnp.dot(left.T, right, preferred_element_type=jnp.float32)


def body(
    block_input,
    out_cotangent,
    w_query,
    w_key,
    w_value,
    w_output,
    bias_query,
    bias_value,
    bias_output,
    gain_first,
    shift_first,
    w_inner,
    bias_inner,
    w_down,
    bias_down,
    gain_second,
    shift_second,
):
    rows = block_input.shape[0]
    width = w_query.shape[1]
    shape4 = (rows // SEQ, SEQ, HEADS, HEAD_DIM)
    wq, wk, wv, wo, bq, bv, bo, gone, sone, wi, bi, wd, bd, gtwo, stwo = (
        lax.all_gather(w_query, "shard", axis=0, tiled=True),
        lax.all_gather(w_key, "shard", axis=0, tiled=True),
        lax.all_gather(w_value, "shard", axis=0, tiled=True),
        lax.all_gather(w_output, "shard", axis=0, tiled=True),
        lax.all_gather(bias_query.astype(jnp.bfloat16), "shard", axis=0, tiled=True).astype(
            bias_query.dtype
        ),
        lax.all_gather(bias_value.astype(jnp.bfloat16), "shard", axis=0, tiled=True).astype(
            bias_value.dtype
        ),
        lax.all_gather(bias_output.astype(jnp.bfloat16), "shard", axis=0, tiled=True).astype(
            bias_output.dtype
        ),
        lax.all_gather(gain_first.astype(jnp.bfloat16), "shard", axis=0, tiled=True).astype(
            gain_first.dtype
        ),
        lax.all_gather(shift_first.astype(jnp.bfloat16), "shard", axis=0, tiled=True).astype(
            shift_first.dtype
        ),
        lax.all_gather(w_inner, "shard", axis=0, tiled=True),
        lax.all_gather(bias_inner.astype(jnp.bfloat16), "shard", axis=0, tiled=True).astype(
            bias_inner.dtype
        ),
        lax.all_gather(w_down, "shard", axis=0, tiled=True),
        lax.all_gather(bias_down.astype(jnp.bfloat16), "shard", axis=0, tiled=True).astype(
            bias_down.dtype
        ),
        lax.all_gather(gain_second.astype(jnp.bfloat16), "shard", axis=0, tiled=True).astype(
            gain_second.dtype
        ),
        lax.all_gather(shift_second.astype(jnp.bfloat16), "shard", axis=0, tiled=True).astype(
            shift_second.dtype
        ),
    )
    query = (jnp.dot(block_input, wq, preferred_element_type=jnp.float32) + bq).astype(jnp.bfloat16)
    keyed = jnp.dot(block_input, wk, preferred_element_type=jnp.float32).astype(jnp.bfloat16)
    valued = (jnp.dot(block_input, wv, preferred_element_type=jnp.float32) + bv).astype(
        jnp.bfloat16
    )
    query4 = query.reshape(shape4).astype(jnp.float32)
    keyed4 = keyed.reshape(shape4).astype(jnp.float32)
    valued4 = valued.reshape(shape4).astype(jnp.float32)
    scores = score_table(query4, keyed4)
    top = jnp.max(scores, axis=-1, keepdims=True)
    logsum = top + jnp.log(jnp.sum(jnp.exp(scores - top), axis=-1, keepdims=True))
    probs_b = jnp.exp(scores - logsum).astype(jnp.bfloat16)
    context4 = jnp.einsum("bhqk,bkhe->bqhe", probs_b.astype(jnp.float32), valued4).astype(
        jnp.bfloat16
    )
    context = context4.reshape(rows, width)
    resid_one = (
        block_input.astype(jnp.float32)
        + jnp.dot(context, wo, preferred_element_type=jnp.float32)
        + bo
    )
    normed_one, rstd_one = norm_parts(resid_one)
    hidden = normed_one * gone + sone
    hidden_b = hidden.astype(jnp.bfloat16)
    inner = jnp.dot(hidden_b, wi, preferred_element_type=jnp.float32) + bi
    acted = gelu_value(inner).astype(jnp.bfloat16)
    resid_two = hidden + jnp.dot(acted, wd, preferred_element_type=jnp.float32) + bd
    normed_two, rstd_two = norm_parts(resid_two)
    output = (normed_two * gtwo + stwo).astype(jnp.bfloat16)
    bwq, bwk, bwv, bwo, bgone, bwi, bwd, bgtwo = (
        lax.all_gather(w_query, "shard", axis=0, tiled=True),
        lax.all_gather(w_key, "shard", axis=0, tiled=True),
        lax.all_gather(w_value, "shard", axis=0, tiled=True),
        lax.all_gather(w_output, "shard", axis=0, tiled=True),
        lax.all_gather(gain_first.astype(jnp.bfloat16), "shard", axis=0, tiled=True).astype(
            gain_first.dtype
        ),
        lax.all_gather(w_inner, "shard", axis=0, tiled=True),
        lax.all_gather(w_down, "shard", axis=0, tiled=True),
        lax.all_gather(gain_second.astype(jnp.bfloat16), "shard", axis=0, tiled=True).astype(
            gain_second.dtype
        ),
    )
    dout = out_cotangent.astype(jnp.float32)
    g_gain_second = jnp.sum(dout * normed_two, axis=0)
    g_shift_second = jnp.sum(dout, axis=0)
    d_two = norm_back(dout * bgtwo, normed_two, rstd_two)
    d_two_b = d_two.astype(jnp.bfloat16)
    g_bias_down = jnp.sum(d_two, axis=0)
    d_inner = jnp.dot(d_two_b, bwd.T, preferred_element_type=jnp.float32) * gelu_slope(inner)
    g_bias_inner = jnp.sum(d_inner, axis=0)
    d_inner_b = d_inner.astype(jnp.bfloat16)
    d_hidden = d_two + jnp.dot(d_inner_b, bwi.T, preferred_element_type=jnp.float32)
    g_gain_first = jnp.sum(d_hidden * normed_one, axis=0)
    g_shift_first = jnp.sum(d_hidden, axis=0)
    d_one = norm_back(d_hidden * bgone, normed_one, rstd_one)
    g_bias_output = jnp.sum(d_one, axis=0)
    d_one_b = d_one.astype(jnp.bfloat16)
    d_context = jnp.dot(d_one_b, bwo.T, preferred_element_type=jnp.float32).astype(jnp.bfloat16)
    d_context4 = d_context.reshape(shape4).astype(jnp.float32)
    probs = jnp.exp(score_table(query4, keyed4) - logsum)
    probs_again = probs.astype(jnp.bfloat16).astype(jnp.float32)
    d_probs = jnp.einsum("bqhe,bkhe->bhqk", d_context4, valued4)
    delta = jnp.sum(probs * d_probs, axis=-1, keepdims=True)
    d_scores = (probs * (d_probs - delta) * 0.125).astype(jnp.bfloat16).astype(jnp.float32)
    d_query = jnp.einsum("bhqk,bkhe->bqhe", d_scores, keyed4).reshape(rows, width)
    d_keyed = jnp.einsum("bhqk,bqhe->bkhe", d_scores, query4).reshape(rows, width)
    d_valued = jnp.einsum("bhqk,bqhe->bkhe", probs_again, d_context4).reshape(rows, width)
    g_bias_query = jnp.sum(d_query, axis=0)
    g_bias_value = jnp.sum(d_valued, axis=0)
    dq_b = d_query.astype(jnp.bfloat16)
    dk_b = d_keyed.astype(jnp.bfloat16)
    dv_b = d_valued.astype(jnp.bfloat16)
    d_input = d_one + jnp.dot(dq_b, bwq.T, preferred_element_type=jnp.float32)
    d_input = d_input + jnp.dot(dk_b, bwk.T, preferred_element_type=jnp.float32)
    d_input = d_input + jnp.dot(dv_b, bwv.T, preferred_element_type=jnp.float32)
    owned = (
        lax.psum_scatter(
            left_product(block_input, dq_b).astype(jnp.bfloat16),
            "shard",
            scatter_dimension=0,
            tiled=True,
        ).astype(jnp.float32),
        lax.psum_scatter(
            left_product(block_input, dk_b).astype(jnp.bfloat16),
            "shard",
            scatter_dimension=0,
            tiled=True,
        ).astype(jnp.float32),
        lax.psum_scatter(
            left_product(block_input, dv_b).astype(jnp.bfloat16),
            "shard",
            scatter_dimension=0,
            tiled=True,
        ).astype(jnp.float32),
        lax.psum_scatter(
            left_product(context, d_one_b).astype(jnp.bfloat16),
            "shard",
            scatter_dimension=0,
            tiled=True,
        ).astype(jnp.float32),
        lax.psum_scatter(
            g_bias_query.astype(jnp.bfloat16), "shard", scatter_dimension=0, tiled=True
        ).astype(jnp.float32),
        lax.psum_scatter(
            g_bias_value.astype(jnp.bfloat16), "shard", scatter_dimension=0, tiled=True
        ).astype(jnp.float32),
        lax.psum_scatter(
            g_bias_output.astype(jnp.bfloat16), "shard", scatter_dimension=0, tiled=True
        ).astype(jnp.float32),
        lax.psum_scatter(
            g_gain_first.astype(jnp.bfloat16), "shard", scatter_dimension=0, tiled=True
        ).astype(jnp.float32),
        lax.psum_scatter(
            g_shift_first.astype(jnp.bfloat16), "shard", scatter_dimension=0, tiled=True
        ).astype(jnp.float32),
        lax.psum_scatter(
            left_product(hidden_b, d_inner_b).astype(jnp.bfloat16),
            "shard",
            scatter_dimension=0,
            tiled=True,
        ).astype(jnp.float32),
        lax.psum_scatter(
            g_bias_inner.astype(jnp.bfloat16), "shard", scatter_dimension=0, tiled=True
        ).astype(jnp.float32),
        lax.psum_scatter(
            left_product(acted, d_two_b).astype(jnp.bfloat16),
            "shard",
            scatter_dimension=0,
            tiled=True,
        ).astype(jnp.float32),
        lax.psum_scatter(
            g_bias_down.astype(jnp.bfloat16), "shard", scatter_dimension=0, tiled=True
        ).astype(jnp.float32),
        lax.psum_scatter(
            g_gain_second.astype(jnp.bfloat16), "shard", scatter_dimension=0, tiled=True
        ).astype(jnp.float32),
        lax.psum_scatter(
            g_shift_second.astype(jnp.bfloat16), "shard", scatter_dimension=0, tiled=True
        ).astype(jnp.float32),
    )
    summed = (
        lax.psum(owned[0].astype(jnp.bfloat16), "rep").astype(jnp.float32),
        lax.psum(owned[1].astype(jnp.bfloat16), "rep").astype(jnp.float32),
        lax.psum(owned[2].astype(jnp.bfloat16), "rep").astype(jnp.float32),
        lax.psum(owned[3].astype(jnp.bfloat16), "rep").astype(jnp.float32),
        lax.psum(owned[4].astype(jnp.bfloat16), "rep").astype(jnp.float32),
        lax.psum(owned[5].astype(jnp.bfloat16), "rep").astype(jnp.float32),
        lax.psum(owned[6].astype(jnp.bfloat16), "rep").astype(jnp.float32),
        lax.psum(owned[7].astype(jnp.bfloat16), "rep").astype(jnp.float32),
        lax.psum(owned[8].astype(jnp.bfloat16), "rep").astype(jnp.float32),
        lax.psum(owned[9].astype(jnp.bfloat16), "rep").astype(jnp.float32),
        lax.psum(owned[10].astype(jnp.bfloat16), "rep").astype(jnp.float32),
        lax.psum(owned[11].astype(jnp.bfloat16), "rep").astype(jnp.float32),
        lax.psum(owned[12].astype(jnp.bfloat16), "rep").astype(jnp.float32),
        lax.psum(owned[13].astype(jnp.bfloat16), "rep").astype(jnp.float32),
        lax.psum(owned[14].astype(jnp.bfloat16), "rep").astype(jnp.float32),
    )
    return (
        output,
        d_input.astype(jnp.bfloat16),
        summed[0],
        summed[1],
        summed[2],
        summed[3],
        summed[4],
        summed[5],
        summed[6],
        summed[7],
        summed[8],
        summed[9],
        summed[10],
        summed[11],
        summed[12],
        summed[13],
        summed[14],
    )


def solution(mesh):
    placed = (
        P(("shard", "rep"), None),
        P(("shard", "rep"), None),
        P("shard", None),
        P("shard", None),
        P("shard", None),
        P("shard", None),
        P("shard"),
        P("shard"),
        P("shard"),
        P("shard"),
        P("shard"),
        P("shard", None),
        P("shard"),
        P("shard", None),
        P("shard"),
        P("shard"),
        P("shard"),
    )
    return jax.shard_map(
        body,
        mesh=mesh,
        in_specs=placed,
        out_specs=(
            P(("shard", "rep"), None),
            P(("shard", "rep"), None),
            P("shard", None),
            P("shard", None),
            P("shard", None),
            P("shard", None),
            P("shard"),
            P("shard"),
            P("shard"),
            P("shard"),
            P("shard"),
            P("shard", None),
            P("shard"),
            P("shard", None),
            P("shard"),
            P("shard"),
            P("shard"),
        ),
        check_vma=False,
    )
```

profile of v0, /device:TPU:0, one launch (start us, length us, event | category | flops | bytes accessed | tf_op | source)
XLA Modules:
  0.0 1153.5 jit_solution(8875397504020877932)
XLA Ops:
  11.3 22.4 %all-gather.1 = bf16[8,1,128]{2,1,0:T(2,128)(2,1)S(1)} all-gather(bf16[1,1,128]{2,1,0:T(2,128)(2,1)S(1)} %convert_bitcast_fusion.9), channel_id=1, replica_groups=mesh['shard'=8,'rep'=4] {'shard'}, dimensions={0}, use_global_device_ids=true | all-gather | bytes 2304 | tf_op jit(solution)/shard_map/all_gather | solution.py:77
  33.8 16.6 %all-gather = bf16[8,1,128]{2,1,0:T(2,128)(2,1)S(1)} all-gather(bf16[1,1,128]{2,1,0:T(2,128)(2,1)S(1)} %convert_bitcast_fusion.10), channel_id=1, replica_groups=mesh['shard'=8,'rep'=4] {'shard'}, dimensions={0}, use_global_device_ids=true | all-gather | bytes 2304 | tf_op jit(solution)/shard_map/all_gather | solution.py:80
  50.3 18.7 %all-gather.2 = bf16[8,1,128]{2,1,0:T(2,128)(2,1)S(1)} all-gather(bf16[1,1,128]{2,1,0:T(2,128)(2,1)S(1)} %convert_bitcast_fusion.8), channel_id=1, replica_groups=mesh['shard'=8,'rep'=4] {'shard'}, dimensions={0}, use_global_device_ids=true | all-gather | bytes 2304 | tf_op jit(solution)/shard_map/all_gather | solution.py:83
  69.0 16.3 %all-gather.3 = bf16[8,1,128]{2,1,0:T(2,128)(2,1)S(1)} all-gather(bf16[1,1,128]{2,1,0:T(2,128)(2,1)S(1)} %convert_bitcast_fusion.7), channel_id=1, replica_groups=mesh['shard'=8,'rep'=4] {'shard'}, dimensions={0}, use_global_device_ids=true | all-gather | bytes 2304 | tf_op jit(solution)/shard_map/all_gather | solution.py:86
  85.3 18.7 %all-gather.4 = bf16[8,1,128]{2,1,0:T(2,128)(2,1)S(1)} all-gather(bf16[1,1,128]{2,1,0:T(2,128)(2,1)S(1)} %convert_bitcast_fusion.6), channel_id=1, replica_groups=mesh['shard'=8,'rep'=4] {'shard'}, dimensions={0}, use_global_device_ids=true | all-gather | bytes 2304 | tf_op jit(solution)/shard_map/all_gather | solution.py:89
  104.1 26.3 %all-gather.5 = bf16[8,1,512]{2,1,0:T(2,128)(2,1)S(1)} all-gather(bf16[1,1,512]{2,1,0:T(2,128)(2,1)S(1)} %reshape.191), channel_id=1, replica_groups=mesh['shard'=8,'rep'=4] {'shard'}, dimensions={0}, use_global_device_ids=true | all-gather | bytes 9216 | tf_op jit(solution)/shard_map/all_gather | solution.py:93
  130.4 16.5 %all-gather.6 = bf16[8,1,128]{2,1,0:T(2,128)(2,1)S(1)} all-gather(bf16[1,1,128]{2,1,0:T(2,128)(2,1)S(1)} %convert_bitcast_fusion.5), channel_id=1, replica_groups=mesh['shard'=8,'rep'=4] {'shard'}, dimensions={0}, use_global_device_ids=true | all-gather | bytes 2304 | tf_op jit(solution)/shard_map/all_gather | solution.py:97
  146.9 18.5 %all-gather.7 = bf16[8,1,128]{2,1,0:T(2,128)(2,1)S(1)} all-gather(bf16[1,1,128]{2,1,0:T(2,128)(2,1)S(1)} %convert_bitcast_fusion.4), channel_id=1, replica_groups=mesh['shard'=8,'rep'=4] {'shard'}, dimensions={0}, use_global_device_ids=true | all-gather | bytes 2304 | tf_op jit(solution)/shard_map/all_gather | solution.py:100
  165.4 16.4 %all-gather.8 = bf16[8,1,128]{2,1,0:T(2,128)(2,1)S(1)} all-gather(bf16[1,1,128]{2,1,0:T(2,128)(2,1)S(1)} %convert_bitcast_fusion.3), channel_id=1, replica_groups=mesh['shard'=8,'rep'=4] {'shard'}, dimensions={0}, use_global_device_ids=true | all-gather | bytes 2304 | tf_op jit(solution)/shard_map/all_gather | solution.py:103
  190.4 21.7 %all-gather.22.cloned.1.call-done = bf16[1024,1024]{1,0:T(8,128)(2,1)} async-done(((bf16[128,1024]{1,0:T(8,128)(2,1)}), bf16[1024,1024]{1,0:T(8,128)(2,1)}) %all-gather.22.cloned.1.call-update) | async-done | bytes 2097168 | tf_op jit(solution)/shard_map/all_gather | solution.py:76
  214.4 122.7 %all-gather.24.cloned.1.call-done = bf16[1024,4096]{1,0:T(8,128)(2,1)} async-done(((bf16[128,4096]{1,0:T(8,128)(2,1)}), bf16[1024,4096]{1,0:T(8,128)(2,1)}) %all-gather.24.cloned.1.call-update) | async-done | bytes 8388624 | tf_op jit(solution)/shard_map/all_gather | solution.py:92
  337.1 4.7 convolution_add_fusion
  341.8 119.9 %all-gather.26.cloned.1.call-done = bf16[4096,1024]{1,0:T(8,128)(2,1)} async-done(((bf16[512,1024]{1,0:T(8,128)(2,1)}), bf16[4096,1024]{1,0:T(8,128)(2,1)}) %all-gather.26.cloned.1.call-update) | async-done | bytes 8388624 | tf_op jit(solution)/shard_map/all_gather | solution.py:96
  461.7 5.0 fusion.55
  468.3 3.3 fusion.58
  471.6 3.0 multiply_reduce_fusion.1
  482.9 3.9 copy.79
  489.4 3.7 convolution_convert_fusion.3
  496.1 4.0 copy.77
  500.2 3.8 fusion.52
  506.9 4.0 copy.75
  513.9 6.9 convolution_convert_fusion.1
  521.9 4.6 convolution_convert_fusion
  526.5 26.9 %reduce-scatter.23.cloned.1.call-done = bf16[128,1024]{1,0:T(8,128)(2,1)} async-done(((bf16[1024,1024]{1,0:T(8,128)(2,1)}), bf16[128,1024]{1,0:T(8,128)(2,1)}) %reduce-scatter.23.cloned.1.call-update) | async-done | bytes 262160
  555.3 69.2 %reduce-scatter.21.cloned.1.call-done = bf16[128,1024]{1,0:T(8,128)(2,1)} async-done(((bf16[1024,1024]{1,0:T(8,128)(2,1)}), bf16[128,1024]{1,0:T(8,128)(2,1)}) %reduce-scatter.21.cloned.1.call-update) | async-done | bytes 262160
  626.3 69.8 %reduce-scatter.19.cloned.1.call-done = bf16[128,1024]{1,0:T(8,128)(2,1)} async-done(((bf16[1024,1024]{1,0:T(8,128)(2,1)}), bf16[128,1024]{1,0:T(8,128)(2,1)}) %reduce-scatter.19.cloned.1.call-update) | async-done | bytes 262160
  697.9 69.6 %reduce-scatter.13.cloned.1.call-done = bf16[128,1024]{1,0:T(8,128)(2,1)} async-done(((bf16[1024,1024]{1,0:T(8,128)(2,1)}), bf16[128,1024]{1,0:T(8,128)(2,1)}) %reduce-scatter.13.cloned.1.call-update) | async-done | bytes 262160 | tf_op jit(solution)/shard_map/reduce_scatter | solution.py:202
  767.5 150.2 %reduce-scatter.15.cloned.1.call-done = bf16[128,4096]{1,0:T(8,128)(2,1)} async-done(((bf16[1024,4096]{1,0:T(8,128)(2,1)}), bf16[128,4096]{1,0:T(8,128)(2,1)}) %reduce-scatter.15.cloned.1.call-update) | async-done | bytes 1048592 | tf_op jit(solution)/shard_map/reduce_scatter | solution.py:223
  917.7 150.1 %reduce-scatter.17.cloned.1.call-done = bf16[512,1024]{1,0:T(8,128)(2,1)} async-done(((bf16[4096,1024]{1,0:T(8,128)(2,1)}), bf16[512,1024]{1,0:T(8,128)(2,1)}) %reduce-scatter.17.cloned.1.call-update) | async-done | bytes 1048592 | tf_op jit(solution)/shard_map/reduce_scatter | solution.py:232
  1070.0 35.2 %all-reduce.9 = (bf16[1024]{0:T(1024)(128)(2,1)S(1)}, bf16[1024]{0:T(1024)(128)(2,1)S(1)}, bf16[1024]{0:T(1024)(128)(2,1)S(1)}, bf16[1024]{0:T(1024)(128)(2,1)S(...) all-reduce(bf16[1024]{0:T(1024)(128)(2,1)S(1)} %convert_element_typ, ...), channel_id=6, replica_groups=mesh['shard'=8,'rep'=4] {'shard'}, use_global_device_ids=true, to_apply=%region_20.0.clone | all-reduce | flops 12288 | bytes 49152
  1105.9 5.7 all-reduce.10
  1121.3 17.5 %all-reduce.14.cloned.1.call-done = (bf16[128,1024]{0,1:T(8,128)(2,1)}, bf16[128,1024]{0,1:T(8,128)(2,1)}, bf16[128,1024]{0,1:T(8,128)(2,1)}, bf16[128,1024]{1,0...) async-done(((bf16[128,1024]{0,1:T(8,128)(2,1)}, bf16[128,1024]{0,1:T(8,128)(2,1)}, bf16[128,1024]{0,1:T(8,128)(2,1)}, bf16[128,1024]{1,0:T(8,128)(2,1)}, ...) | async-done | bytes 3145744 | tf_op jit(solution)/shard_map/psum | solution.py:249
  (191 shorter events, 61.8 us)
Async XLA Ops:
  7.2 26.5 %copy-start.26 = (f32[128]{0:T(128)S(1)}, f32[128]{0:T(128)}, u32[]{:S(2)}) copy-start(f32[128]{0:T(128)} %param.24) | copy-start | bytes 1540
  7.2 43.1 %copy-start.27 = (f32[128]{0:T(128)S(1)}, f32[128]{0:T(128)}, u32[]{:S(2)}) copy-start(f32[128]{0:T(128)} %param.25) | copy-start | bytes 1540
  7.2 61.8 %copy-start.28 = (f32[128]{0:T(128)S(1)}, f32[128]{0:T(128)}, u32[]{:S(2)}) copy-start(f32[128]{0:T(128)} %param.26) | copy-start | bytes 1540
  7.2 78.1 %copy-start.29 = (f32[128]{0:T(128)S(1)}, f32[128]{0:T(128)}, u32[]{:S(2)}) copy-start(f32[128]{0:T(128)} %param.27) | copy-start | bytes 1540
  7.2 96.8 %copy-start.24 = (f32[512]{0:T(512)S(1)}, f32[512]{0:T(512)}, u32[]{:S(2)}) copy-start(f32[512]{0:T(512)} %param.29) | copy-start | bytes 6148
  7.3 123.1 %copy-start.30 = (f32[128]{0:T(128)S(1)}, f32[128]{0:T(128)}, u32[]{:S(2)}) copy-start(f32[128]{0:T(128)} %param.31) | copy-start | bytes 1540
  7.3 139.6 %copy-start.31 = (f32[128]{0:T(128)S(1)}, f32[128]{0:T(128)}, u32[]{:S(2)}) copy-start(f32[128]{0:T(128)} %param.32) | copy-start | bytes 1540
  7.3 158.1 %copy-start.32 = (f32[128]{0:T(128)S(1)}, f32[128]{0:T(128)}, u32[]{:S(2)}) copy-start(f32[128]{0:T(128)} %param.33) | copy-start | bytes 1540
  7.3 174.5 %copy-start.1 = (bf16[128,1024]{1,0:T(8,128)(2,1)S(1)}, bf16[128,1024]{1,0:T(8,128)(2,1)}, u32[]{:S(2)}) copy-start(bf16[128,1024]{1,0:T(8,128)(2,1)} %param.17) | copy-start | bytes 786436
  7.3 174.5 %all-gather.18.cloned.1.call-start = ((), (), s32[]{:S(2)}) async-start(), calls=%async_computation.7 | async-start | bytes 2359296 | tf_op jit(solution)/shard_map/all_gather | solution.py:73
  8.0 176.0 %all-gather.20.cloned.1.call-start = ((), (), s32[]{:S(2)}) async-start(), calls=%async_computation.8 | async-start | bytes 2359296 | tf_op jit(solution)/shard_map/all_gather | solution.py:74
  8.8 177.6 %all-gather.16.cloned.1.call-start = ((), (), s32[]{:S(2)}) async-start(), calls=%async_computation.6 | async-start | bytes 2359296 | tf_op jit(solution)/shard_map/all_gather | solution.py:75
  9.5 202.5 %all-gather.22.cloned.1.call-start = ((), (), s32[]{:S(2)}) async-start(), calls=%async_computation.9 | async-start | bytes 2359296 | tf_op jit(solution)/shard_map/all_gather | solution.py:76
  10.1 327.0 %all-gather.24.cloned.1.call-start = ((), (), s32[]{:S(2)}) async-start(), calls=%async_computation.10 | async-start | bytes 9437184 | tf_op jit(solution)/shard_map/all_gather | solution.py:92
  10.7 451.1 %all-gather.26.cloned.1.call-start = ((), (), s32[]{:S(2)}) async-start(), calls=%async_computation.11 | async-start | bytes 9437184 | tf_op jit(solution)/shard_map/all_gather | solution.py:96
  11.3 542.2 %reduce-scatter.23.cloned.1.call-start = ((), (), s32[]{:S(2)}) async-start(), calls=%async_computation.17 | async-start | bytes 2359296
  184.0 4.7 copy-start.18
  190.4 146.7 %copy-start.14 = (bf16[16,64,128]{2,1,0:T(8,128)(2,1)}, bf16[16,64,128]{2,1,0:T(8,128)(2,1)S(1)}, u32[]{:S(2)}) copy-start(bf16[16,64,128]{2,1,0:T(8,128)(2,1)S(1)} %convolution_convert_fusion.5) | copy-start | bytes 786436
  461.7 6.5 slice-start.2
  461.7 5.3 copy-start.11
  461.7 6.5 slice-start.3
  486.8 137.7 %reduce-scatter.21.cloned.1.call-start = ((), (), s32[]{:S(2)}) async-start(), calls=%async_computation.16 | async-start | bytes 2359296
  500.1 196.0 %reduce-scatter.19.cloned.1.call-start = ((), (), s32[]{:S(2)}) async-start(), calls=%async_computation.15 | async-start | bytes 2359296
  510.9 256.6 %reduce-scatter.13.cloned.1.call-start = ((), (), s32[]{:S(2)}) async-start(), calls=%async_computation.12 | async-start | bytes 2359296 | tf_op jit(solution)/shard_map/reduce_scatter | solution.py:202
  513.9 403.8 %reduce-scatter.15.cloned.1.call-start = ((), (), s32[]{:S(2)}) async-start(), calls=%async_computation.13 | async-start | bytes 9437184 | tf_op jit(solution)/shard_map/reduce_scatter | solution.py:223
  520.9 546.9 %reduce-scatter.17.cloned.1.call-start = ((), (), s32[]{:S(2)}) async-start(), calls=%async_computation.14 | async-start | bytes 9437184 | tf_op jit(solution)/shard_map/reduce_scatter | solution.py:232
  526.5 612.4 %all-reduce.14.cloned.1.call-start = ((), (), s32[]{:S(2)}) async-start(), calls=%async_computation.18 | async-start | bytes 6291456 | tf_op jit(solution)/shard_map/psum | solution.py:249
  555.3 512.5 %copy-start.12 = (bf16[128,1024]{1,0:T(8,128)(2,1)S(1)}, bf16[128,1024]{1,0:T(8,128)(2,1)}, u32[]{:S(2)}) copy-start(bf16[128,1024]{1,0:T(8,128)(2,1)} %param.18) | copy-start | bytes 786436
  626.3 441.6 %copy-start.33 = (u32[32]{0:T(128)S(1)}, u32[32]{0:T(128)}, u32[]{:S(2)}) copy-start(u32[32]{0:T(128)} %constant.32) | copy-start | bytes 388
  626.3 490.0 %copy-start.3 = (bf16[1024,1024]{1,0:T(8,128)(2,1)S(1)}, bf16[1024,1024]{1,0:T(8,128)(2,1)}, u32[]{:S(2)}) copy-start(bf16[1024,1024]{1,0:T(8,128)(2,1)} %all-gather.18.cloned.1.call-done) | copy-start | bytes 6291460
  1067.8 50.3 %copy-start.19 = (bf16[16,64,128]{2,1,0:T(8,128)(2,1)S(1)}, bf16[16,64,128]{2,1,0:T(8,128)(2,1)}, u32[]{:S(2)}) copy-start(bf16[16,64,128]{2,1,0:T(8,128)(2,1)} %convolution_convert_fusion.3) | copy-start | bytes 786436
  1111.6 6.5 copy-start.4
  (19 other events, 47.3 us)
Sparse Core Ops, SparseCore 0:
  10.2 51.9 all-gather.17
  64.4 47.8 all-gather.19
  114.4 47.8 all-gather.15
  164.3 47.7 all-gather.21
  214.0 122.9 all-gather.23
  339.0 122.6 all-gather.25
  486.9 66.5 reduce-scatter.22
  557.0 67.4 reduce-scatter.20
  628.6 67.4 reduce-scatter.18
  700.1 67.4 reduce-scatter.12
  771.2 146.4 reduce-scatter.14
  921.2 146.5 reduce-scatter.16
  1071.1 67.6 all-reduce.13
where the time goes:
time: 1150 us
  waiting for transfers between devices  821 us (71%)
  blocking collectives  211 us (18%)
  matrix products  64.1 us (6%)
  local copies, waits for them, and re-layouts  28.1 us (2%)
  between operations  15.9 us (1%)
  other arithmetic  12.1 us (1%)
    unnamed x16, waiting for transfers between devices  170 us
    reduce_scatter x1, waiting for transfers between devices, body(): lax.psum_scatter(left_product(hidden_b, d_inner_b).astype(jnp.bfloat16),...  150 us
    reduce_scatter x1, waiting for transfers between devices, body(): lax.psum_scatter(left_product(acted, d_two_b).astype(jnp.bfloat16), 'shar...  150 us
    all_gather x1, waiting for transfers between devices, body(): lax.all_gather(w_inner, 'shard', axis=0, tiled=True)  123 us
    all_gather x1, waiting for transfers between devices, body(): lax.all_gather(w_down, 'shard', axis=0, tiled=True)  120 us
    reduce_scatter x1, waiting for transfers between devices, body(): lax.psum_scatter(left_product(context, d_one_b).astype(jnp.bfloat16), 'sh...  69.6 us
    unnamed x1, blocking collectives  35.2 us
    all_gather x1, blocking collectives, body(): lax.all_gather(bias_inner.astype(jnp.bfloat16), 'shard', axis=0, tiled=True)  26.3 us
  transfers between devices with their start and end apart: 13, of which 10 were waited for; matrix products, arithmetic and copies ran while one was open for 6% of the time, Pallas kernels for 0%

commit v1 on v0

v1 whole, which is shorter than its diff:
```python
import jax
import jax.numpy as jnp
from jax import lax
from jax.sharding import PartitionSpec as P

HEAD_DIM = 64
SEQ = 128
PAD = 16


EPS = 1e-06
INV_ROOT_TWO = 0.7071067811865476
INV_ROOT_TWO_PI = 0.3989422804014327
BF = jnp.bfloat16
F32 = jnp.float32


def norm_parts(resid):
    centre = resid - jnp.mean(resid, axis=-1, keepdims=True)
    variance = jnp.mean(centre * centre, axis=-1, keepdims=True)
    rstd = lax.rsqrt(variance + EPS)
    return (centre * rstd, rstd)


def norm_back(upstream, normed, rstd):
    return rstd * (
        upstream
        - jnp.mean(upstream, axis=-1, keepdims=True)
        - normed * jnp.mean(upstream * normed, axis=-1, keepdims=True)
    )


def mm(a, b):
    return jnp.dot(a, b, preferred_element_type=F32)


def mm_nt(a, b):
    return lax.dot_general(a, b, (((1,), (1,)), ((), ())), preferred_element_type=F32)


def mm_tn(a, b):
    return lax.dot_general(a, b, (((0,), (0,)), ((), ())), preferred_element_type=F32)


def ein(spec, a, b):
    return jnp.einsum(spec, a, b, preferred_element_type=F32)


def gather_rep(block):
    return lax.all_gather(block, "rep", axis=0, tiled=True)


def scatter_rep(partial):
    return lax.psum_scatter(partial, "rep", scatter_dimension=0, tiled=True).astype(F32)


def norm_one_step(partial, x, bo, gone, sone):
    resid = x.astype(F32) + scatter_rep(partial) + bo
    normed, rstd = norm_parts(resid)
    hidden = normed * gone + sone
    return normed, rstd, hidden, gather_rep(hidden.astype(BF))


def norm_two_step(partial, hidden, bd, gtwo, stwo, cot):
    normed, rstd = norm_parts(hidden + scatter_rep(partial) + bd)
    output = (normed * gtwo + stwo).astype(BF)
    dout = cot.astype(F32)
    d_two = norm_back(dout * gtwo, normed, rstd)
    sums = (jnp.sum(d_two, 0), jnp.sum(dout * normed, 0), jnp.sum(dout, 0))
    return output, d_two, sums, gather_rep(d_two.astype(BF))


def back_one_step(partial, d_two, normed, rstd, gone):
    d_hidden = d_two + scatter_rep(partial)
    d_one = norm_back(d_hidden * gone, normed, rstd)
    sums = (jnp.sum(d_one, 0), jnp.sum(d_hidden * normed, 0), jnp.sum(d_hidden, 0))
    return d_one, sums, gather_rep(d_one.astype(BF))


def body(
    block_input,
    out_cotangent,
    w_query,
    w_key,
    w_value,
    w_output,
    bias_query,
    bias_value,
    bias_output,
    gain_first,
    shift_first,
    w_inner,
    bias_inner,
    w_down,
    bias_down,
    gain_second,
    shift_second,
):
    S = lax.axis_size("shard")
    R = lax.axis_size("rep")
    r = lax.axis_index("rep")
    T = block_input.shape[0]
    D = w_query.shape[1]
    ds = w_query.shape[0]
    dr = D // R
    fs = w_down.shape[0]
    fr = fs // R
    W = 4 * dr

    def cols(w):
        return lax.dynamic_slice(w, (0, r * dr), (ds, dr))

    small = jnp.concatenate(
        [
            v.astype(BF)
            for v in (
                bias_query,
                bias_value,
                bias_output,
                gain_first,
                shift_first,
                bias_down,
                gain_second,
                shift_second,
                bias_inner,
            )
        ]
    )
    n_small = small.shape[0]
    small = jnp.pad(small, (0, PAD * W - n_small)).reshape(PAD, W)
    pack = jnp.concatenate(
        [jnp.concatenate([cols(w_query), cols(w_key), cols(w_value), cols(w_output)], 1), small], 0
    )
    got = lax.all_gather(pack, "shard", axis=0)
    x_all = gather_rep(block_input)
    wi_r = lax.dynamic_index_in_dim(w_inner.reshape(ds, S, R, fr), r, 2, keepdims=False)
    wi = lax.all_gather(wi_r.reshape(ds, S * fr), "shard", axis=0, tiled=True)
    wd = lax.all_gather(
        lax.dynamic_slice(w_down, (r * fr, 0), (fr, D)), "shard", axis=0, tiled=True
    )
    wqkv = got[:, :ds, : 3 * dr].reshape(D, 3 * dr)
    wo = lax.all_to_all(
        got[:, :ds, 3 * dr :].reshape(D, dr), "rep", split_axis=0, concat_axis=1, tiled=True
    )
    flat = got[:, ds:, :].reshape(S, PAD * W)[:, :n_small].astype(F32)
    bq, bv, bo, gone, sone, bd, gtwo, stwo = (
        flat[:, i * ds : (i + 1) * ds].reshape(D) for i in range(8)
    )
    bi = lax.dynamic_index_in_dim(flat[:, 8 * ds :].reshape(S, R, fr), r, 1, keepdims=False)
    bi = bi.reshape(S * fr)
    bq = lax.dynamic_slice(bq, (r * dr,), (dr,))
    bv = lax.dynamic_slice(bv, (r * dr,), (dr,))

    N = R * T
    shape4 = (N // SEQ, SEQ, dr // HEAD_DIM, HEAD_DIM)
    qkv = mm(x_all, wqkv)
    query = (qkv[:, :dr] + bq).astype(BF).reshape(shape4)
    keyed = qkv[:, dr : 2 * dr].astype(BF).reshape(shape4)
    valued = (qkv[:, 2 * dr :] + bv).astype(BF).reshape(shape4)
    scores = ein("bqhe,bkhe->bhqk", query, keyed) * 0.125
    top = jnp.max(scores, axis=-1, keepdims=True)
    logsum = top + jnp.log(jnp.sum(jnp.exp(scores - top), axis=-1, keepdims=True))
    probs = jnp.exp(scores - logsum)
    probs_b = probs.astype(BF)
    context = ein("bhqk,bkhe->bqhe", probs_b, valued).astype(BF).reshape(N, dr)
    attn_part = mm(context, wo).astype(BF)

    normed_one, rstd_one, hidden, hidden_all = norm_one_step(attn_part, block_input, bo, gone, sone)
    inner = mm(hidden_all, wi) + bi
    phi = 0.5 * (1.0 + lax.erf(inner * INV_ROOT_TWO))
    acted = (inner * phi).astype(BF)
    slope = phi + inner * jnp.exp(-0.5 * inner * inner) * INV_ROOT_TWO_PI
    down_part = mm(acted, wd).astype(BF)

    output, d_two, sums_two, d_two_all = norm_two_step(
        down_part, hidden, bd, gtwo, stwo, out_cotangent
    )
    d_inner = mm_nt(d_two_all, wd) * slope
    g_bias_inner = jnp.sum(d_inner, axis=0)
    d_inner_b = d_inner.astype(BF)
    hid_part = mm_nt(d_inner_b, wi).astype(BF)
    g_wd = lax.psum_scatter(
        mm_tn(acted, d_two_all).astype(BF), "shard", scatter_dimension=0, tiled=True
    )
    g_wi = lax.psum_scatter(
        mm_tn(hidden_all, d_inner_b).astype(BF), "shard", scatter_dimension=0, tiled=True
    )

    d_one, sums_one, d_one_all = back_one_step(hid_part, d_two, normed_one, rstd_one, gone)
    g_wo = mm_tn(context, d_one_all).astype(BF)
    g_wo = lax.all_to_all(g_wo, "rep", split_axis=1, concat_axis=0, tiled=True)
    d_context = mm_nt(d_one_all, wo).astype(BF).reshape(shape4)
    d_probs = ein("bqhe,bkhe->bhqk", d_context, valued)
    delta = jnp.sum(probs * d_probs, axis=-1, keepdims=True)
    d_scores = (probs * (d_probs - delta) * 0.125).astype(BF)
    d_query = ein("bhqk,bkhe->bqhe", d_scores, keyed).reshape(N, dr)
    d_keyed = ein("bhqk,bqhe->bkhe", d_scores, query).reshape(N, dr)
    d_valued = ein("bhqk,bqhe->bkhe", probs_b, d_context).reshape(N, dr)
    g_bias_query = jnp.sum(d_query, axis=0)
    g_bias_value = jnp.sum(d_valued, axis=0)
    d_qkv = jnp.concatenate([d_query.astype(BF), d_keyed.astype(BF), d_valued.astype(BF)], 1)
    in_part = mm_nt(d_qkv, wqkv).astype(BF)

    def placed(v):
        return lax.dynamic_update_slice(jnp.zeros((D,), F32), v, (r * dr,)).reshape(S, ds)

    g_small = jnp.concatenate(
        [
            placed(g_bias_query),
            placed(g_bias_value),
            sums_one[0].reshape(S, ds),
            sums_one[1].reshape(S, ds),
            sums_one[2].reshape(S, ds),
            sums_two[0].reshape(S, ds),
            sums_two[1].reshape(S, ds),
            sums_two[2].reshape(S, ds),
            g_bias_inner.reshape(S, fr),
        ],
        1,
    ).astype(BF)
    n_g = g_small.shape[1]
    g_small = jnp.pad(g_small, ((0, 0), (0, PAD * W - n_g))).reshape(S, PAD, W)
    g_pack = jnp.concatenate([mm_tn(x_all, d_qkv).astype(BF), g_wo], 1).reshape(S, ds, W)
    g_pack = jnp.concatenate([g_pack, g_small], 1)
    g_pack = lax.psum_scatter(g_pack, "shard", scatter_dimension=0, tiled=True)[0]

    grad_input = (d_one + scatter_rep(in_part)).astype(BF)

    wd_out = gather_rep(g_wd).astype(F32)
    wi_out = lax.all_gather(g_wi, "rep", axis=0).astype(F32)
    wi_out = wi_out.reshape(R, ds, S, fr).transpose(1, 2, 0, 3).reshape(ds, S * R * fr)
    packs = lax.all_gather(g_pack, "rep", axis=0).astype(F32)
    main = packs[:, :ds].reshape(R, ds, 4, dr).transpose(2, 1, 0, 3).reshape(4, ds, D)
    tail = packs[:, ds:].reshape(R, PAD * W)
    summed = jnp.sum(tail[:, : 8 * ds], axis=0)
    gbq, gbv, gbo, ggone, gsone, gbd, ggtwo, gstwo = (
        summed[i * ds : (i + 1) * ds] for i in range(8)
    )
    gbi = tail[:, 8 * ds : n_g].reshape(fs)
    return (
        output,
        grad_input,
        main[0],
        main[1],
        main[2],
        main[3],
        gbq,
        gbv,
        gbo,
        ggone,
        gsone,
        wi_out,
        gbi,
        wd_out,
        gbd,
        ggtwo,
        gstwo,
    )


def solution(mesh):
    tokens = P(("shard", "rep"), None)
    mat = P("shard", None)
    vec = P("shard")
    params = (mat, mat, mat, mat, vec, vec, vec, vec, vec, mat, vec, mat, vec, vec, vec)
    return jax.shard_map(
        body,
        mesh=mesh,
        in_specs=(tokens, tokens) + params,
        out_specs=(tokens, tokens) + params,
        check_vma=False,
    )
```

time: 1150 us -> 669 us (0.58)
  waiting for transfers between devices: 821 us -> 530 us
  blocking collectives: 211 us -> 0 us
  matrix products: 64.1 us -> 45 us
  local copies, waits for them, and re-layouts: 28.1 us -> 43.3 us
  other arithmetic: 12.1 us -> 26.7 us
    all_gather x9 -> x0, blocking collectives: 170 us -> none  [the longest x1 26.3 us: body(): lax.all_gather(bias_inner.astype(jnp.bfloat16), 'shard', axis=0, tiled=True)]
    unnamed x16 -> x17, waiting for transfers between devices: 170 us -> 0.96 us
    reduce_scatter x3 -> x7, waiting for transfers between devices: 370 us -> 279 us  [the longest x4 96.5 us: scatter_rep(): lax.psum_scatter(partial, 'rep', scatter_dimension=0, tiled=True)]
    unnamed x1 -> x0, blocking collectives: 35.2 us -> none
    dot_general x24 -> x18, matrix products: 64.1 us -> 45 us  [the longest x4 13 us: mm(): return jnp.dot(a, b, preferred_element_type=F32)]
    psum x1 -> x0, waiting for transfers between devices: 17.5 us -> none  [body(): lax.psum(owned[0].astype(jnp.bfloat16), 'rep').astype(jnp.float32)]
    all_gather x6 -> x10, waiting for transfers between devices: 264 us -> 248 us  [the longest x5 67 us: gather_rep(): return lax.all_gather(block, 'rep', axis=0, tiled=True)]
    unnamed x96 -> x71, local copies, waits for them, and re-layouts: 25.6 us -> 14.3 us
  transfers between devices with their start and end apart: 13 -> 19, of which waited for: 10 -> 18; matrix products, arithmetic and copies ran while one was open for 6% -> 10% of each run, Pallas kernels for 0% -> 0%
where the time goes in v1:
time: 669 us; the launch traced here: 668 us
  waiting for transfers between devices  530 us (79%)
  matrix products  45 us (7%)
  local copies, waits for them, and re-layouts  43.3 us (6%)
  other arithmetic  26.7 us (4%)
  between operations  14.6 us (2%)
  starting transfers between devices  8.06 us (1%)
    reduce_scatter x4, waiting for transfers between devices, scatter_rep(): lax.psum_scatter(partial, 'rep', scatter_dimension=0, tiled=True)  96.5 us
    reduce_scatter x1, waiting for transfers between devices, body(): lax.psum_scatter(g_pack, 'shard', scatter_dimension=0, tiled=True)[0]  72.1 us
    reduce_scatter x1, waiting for transfers between devices, body(): lax.psum_scatter(mm_tn(acted, d_two_all).astype(BF), 'shard', scatter_dim...  71.2 us
    all_gather x5, waiting for transfers between devices, gather_rep(): return lax.all_gather(block, 'rep', axis=0, tiled=True)  67 us
    all_gather x1, waiting for transfers between devices, body(): got = lax.all_gather(pack, 'shard', axis=0)  53.9 us
    all_gather x1, waiting for transfers between devices, body(): wi = lax.all_gather(wi_r.reshape(ds, S * fr), 'shard', axis=0, tiled=True)  47.8 us
    all_gather x1, waiting for transfers between devices, body(): lax.all_gather(lax.dynamic_slice(w_down, (r * fr, 0), (fr, D)), 'shard',...  46.6 us
    reduce_scatter x1, waiting for transfers between devices, body(): lax.psum_scatter(mm_tn(hidden_all, d_inner_b).astype(BF), 'shard', scatte...  39.4 us
  transfers between devices with their start and end apart: 19, of which 18 were waited for; matrix products, arithmetic and copies ran while one was open for 10% of the time, Pallas kernels for 0%

profile of v1, /device:TPU:0, one launch (start us, length us, event | category | flops | bytes accessed | tf_op | source)
XLA Modules:
  0.0 667.9 jit_solution(12812562725722283410)
XLA Ops:
  18.3 53.9 %all-gather.29.cloned.1.call-done = bf16[1152,1024]{1,0:T(8,128)(2,1)} async-done(((bf16[144,1024]{1,0:T(8,128)(2,1)}), bf16[1152,1024]{1,0:T(8,128)(2,1)}) %all-gather.29.cloned.1.call-update) | async-done | bytes 2359312 | tf_op jit(solution)/shard_map/all_gather | solution.py:134
  77.0 3.5 all-to-all-start
  80.7 12.4 %all-gather.13.cloned.1.call-done = bf16[512,1024]{1,0:T(8,128)(2,1)} async-done(((bf16[128,1024]{1,0:T(8,128)(2,1)}), bf16[512,1024]{1,0:T(8,128)(2,1)}) %all-gather.13.cloned.1.call-update) | async-done | bytes 1048592 | tf_op jit(solution)/shard_map/all_gather | solution.py:50
  93.0 2.2 convolution_bitcast_fusion
  102.9 2.3 copy.99
  106.9 21.8 %reduce-scatter.8.cloned.1.call-done = bf16[128,1024]{1,0:T(8,128)(2,1)} async-done(((bf16[512,1024]{1,0:T(8,128)(2,1)}), bf16[128,1024]{1,0:T(8,128)(2,1)}) %reduce-scatter.8.cloned.1.call-update) | async-done | bytes 262160 | tf_op jit(solution)/shard_map/reduce_scatter | solution.py:54
  133.7 47.8 %all-gather.17.cloned.1.call-done = bf16[1024,1024]{0,1:T(8,128)(2,1)} async-done(((bf16[128,1024]{0,1:T(8,128)(2,1)}), bf16[1024,1024]{0,1:T(8,128)(2,1)}) %all-gather.17.cloned.1.call-update) | async-done | bytes 2097168 | tf_op jit(solution)/shard_map/all_gather | solution.py:137
  181.6 16.9 %all-gather.15.cloned.1.call-done = bf16[512,1024]{1,0:T(8,128)(2,1)} async-done(((bf16[128,1024]{1,0:T(8,128)(2,1)}), bf16[512,1024]{1,0:T(8,128)(2,1)}) %all-gather.15.cloned.1.call-update) | async-done | bytes 1048592 | tf_op jit(solution)/shard_map/all_gather | solution.py:50
  198.5 5.1 multiply_convert_fusion
  203.6 46.6 %all-gather.19.cloned.1.call-done = bf16[1024,1024]{1,0:T(8,128)(2,1)} async-done(((bf16[128,1024]{1,0:T(8,128)(2,1)}), bf16[1024,1024]{1,0:T(8,128)(2,1)}) %all-gather.19.cloned.1.call-update) | async-done | bytes 2097168 | tf_op jit(solution)/shard_map/all_gather | solution.py:138
  250.1 4.2 convolution_convert_fusion.5
  254.4 23.4 %reduce-scatter.10.cloned.1.call-done = bf16[128,1024]{1,0:T(8,128)(2,1)} async-done(((bf16[512,1024]{1,0:T(8,128)(2,1)}), bf16[128,1024]{1,0:T(8,128)(2,1)}) %reduce-scatter.10.cloned.1.call-update) | async-done | bytes 262160 | tf_op jit(solution)/shard_map/reduce_scatter | solution.py:54
  280.9 16.6 %all-gather.21.cloned.1.call-done = bf16[512,1024]{1,0:T(8,128)(2,1)} async-done(((bf16[128,1024]{1,0:T(8,128)(2,1)}), bf16[512,1024]{1,0:T(8,128)(2,1)}) %all-gather.21.cloned.1.call-update) | async-done | bytes 1048592 | tf_op jit(solution)/shard_map/all_gather | solution.py:50
  297.5 4.6 fusion.66
  303.1 2.2 convolution_convert_fusion.4
  305.4 24.9 %reduce-scatter.12.cloned.1.call-done = bf16[128,1024]{1,0:T(8,128)(2,1)} async-done(((bf16[512,1024]{1,0:T(8,128)(2,1)}), bf16[128,1024]{1,0:T(8,128)(2,1)}) %reduce-scatter.12.cloned.1.call-update) | async-done | bytes 262160 | tf_op jit(solution)/shard_map/reduce_scatter | solution.py:54
  333.7 4.2 convolution_convert_fusion.1
  338.0 4.2 convolution_convert_fusion
  342.2 8.3 %all-gather.23.cloned.1.call-done = bf16[512,1024]{1,0:T(8,128)(2,1)} async-done(((bf16[128,1024]{1,0:T(8,128)(2,1)}), bf16[512,1024]{1,0:T(8,128)(2,1)}) %all-gather.23.cloned.1.call-update) | async-done | bytes 1048592 | tf_op jit(solution)/shard_map/all_gather | solution.py:50
  350.5 2.4 convolution_convert_fusion.9
  355.8 2.2 fusion.61
  358.9 2.9 fusion.12
  365.9 3.5 all-to-all-start.1
  371.0 3.4 fusion.6
  383.6 39.4 %reduce-scatter.18.cloned.1.call-done = bf16[128,1024]{1,0:T(8,128)(2,1)} async-done(((bf16[1024,1024]{1,0:T(8,128)(2,1)}), bf16[128,1024]{1,0:T(8,128)(2,1)}) %reduce-scatter.18.cloned.1.call-update) | async-done | bytes 262160 | tf_op jit(solution)/shard_map/reduce_scatter | solution.py:185
  423.1 71.2 %reduce-scatter.20.cloned.1.call-done = bf16[128,1024]{1,0:T(8,128)(2,1)} async-done(((bf16[1024,1024]{1,0:T(8,128)(2,1)}), bf16[128,1024]{1,0:T(8,128)(2,1)}) %reduce-scatter.20.cloned.1.call-update) | async-done | bytes 262160 | tf_op jit(solution)/shard_map/reduce_scatter | solution.py:182
  494.4 72.1 %reduce-scatter.16.cloned.1.call-done = bf16[1,144,1024]{2,1,0:T(8,128)(2,1)} async-done(((bf16[8,144,1024]{2,1,0:T(8,128)(2,1)}), bf16[1,144,1024]{2,1,0:T(8,128)(2,1)}) %reduce-scatter.16.cloned.1.call-update) | async-done | bytes 294928 | tf_op jit(solution)/shard_map/reduce_scatter | solution.py:225
  566.5 26.4 %reduce-scatter.14.cloned.1.call-done = bf16[128,1024]{1,0:T(8,128)(2,1)} async-done(((bf16[512,1024]{1,0:T(8,128)(2,1)}), bf16[128,1024]{1,0:T(8,128)(2,1)}) %reduce-scatter.14.cloned.1.call-update) | async-done | bytes 262160 | tf_op jit(solution)/shard_map/reduce_scatter | solution.py:54
  594.6 16.4 %all-gather.31.cloned.1.call-done = bf16[512,1024]{1,0:T(8,128)(2,1)} async-done(((bf16[128,1024]{1,0:T(8,128)(2,1)}), bf16[512,1024]{1,0:T(8,128)(2,1)}) %all-gather.31.cloned.1.call-update) | async-done | bytes 1048592 | tf_op jit(solution)/shard_map/all_gather | solution.py:230
  616.4 12.8 %all-gather.27.cloned.1.call-done = bf16[512,1024]{1,0:T(8,128)(2,1)} async-done(((bf16[128,1024]{1,0:T(8,128)(2,1)}), bf16[512,1024]{1,0:T(8,128)(2,1)}) %all-gather.27.cloned.1.call-update) | async-done | bytes 1048592 | tf_op jit(solution)/shard_map/all_gather | solution.py:50
  629.2 2.8 convert_element_type.198
  632.0 16.1 %all-gather.25.cloned.1.call-done = bf16[4,144,1024]{2,1,0:T(8,128)(2,1)} async-done(((bf16[1,144,1024]{2,1,0:T(8,128)(2,1)}), bf16[4,144,1024]{2,1,0:T(8,128)(2,1)}) %all-gather.25.cloned.1.call-update) | async-done | bytes 1179664 | tf_op jit(solution)/shard_map/all_gather | solution.py:232
  (199 shorter events, 76.7 us)
Async XLA Ops:
  7.2 125.7 %copy-start = (bf16[512,1024]{1,0:T(8,128)(2,1)S(1)}, bf16[512,1024]{1,0:T(8,128)(2,1)}, u32[]{:S(2)}) copy-start(bf16[512,1024]{1,0:T(8,128)(2,1)} %param.30) | copy-start | bytes 3145732
  7.2 65.0 %all-gather.29.cloned.1.call-start = ((), (), s32[]{:S(2)}) async-start(), calls=%async_computation.24 | async-start | bytes 2654208 | tf_op jit(solution)/shard_map/all_gather | solution.py:134
  17.5 75.5 %all-gather.13.cloned.1.call-start = ((), (), s32[]{:S(2)}) async-start(), calls=%async_computation.9 | async-start | bytes 1310720 | tf_op jit(solution)/shard_map/all_gather | solution.py:50
  75.6 19.7 %copy-start.9 = (bf16[8,128,768]{2,1,0:T(8,128)(2,1)}, bf16[8,128,768]{2,1,0:T(8,128)(2,1)S(1)}, u32[]{:S(2)}) copy-start(bf16[8,128,768]{2,1,0:T(8,128)(2,1)S(1)} %slice.133) | copy-start | bytes 4718596
  77.0 21.6 %all-to-all-start = ((bf16[4,256,256]{2,1,0:T(8,128)(2,1)}), bf16[4,256,256]{2,1,0:T(8,128)(2,1)S(1)}, u32[]{:S(2)}, u32[]{:S(2)}) async-start(bf16[4,256,256]{2,1,0:T(8,128)(2,1)} %bitcast.6), calls=%async_computation | async-start | bytes 1048576 | tf_op jit(solution)/shard_map/all_to_all | solution.py:142
  80.5 48.2 %reduce-scatter.8.cloned.1.call-start = ((), (), s32[]{:S(2)}) async-start(), calls=%async_computation.10 | async-start | bytes 1310720 | tf_op jit(solution)/shard_map/reduce_scatter | solution.py:54
  102.8 25.9 %copy-start.2 = (bf16[128,1024]{1,0:T(8,128)(2,1)S(1)}, bf16[128,1024]{1,0:T(8,128)(2,1)}, u32[]{:S(2)}) copy-start(bf16[128,1024]{1,0:T(8,128)(2,1)} %param.17) | copy-start | bytes 786436
  102.9 78.7 %all-gather.17.cloned.1.call-start = ((), (), s32[]{:S(2)}) async-start(), calls=%async_computation.12 | async-start | bytes 2359296 | tf_op jit(solution)/shard_map/all_gather | solution.py:137
  106.9 91.6 %all-gather.15.cloned.1.call-start = ((), (), s32[]{:S(2)}) async-start(), calls=%async_computation.11 | async-start | bytes 1310720 | tf_op jit(solution)/shard_map/all_gather | solution.py:50
  132.8 117.3 %all-gather.19.cloned.1.call-start = ((), (), s32[]{:S(2)}) async-start(), calls=%async_computation.13 | async-start | bytes 2359296 | tf_op jit(solution)/shard_map/all_gather | solution.py:138
  133.6 144.1 %reduce-scatter.10.cloned.1.call-start = ((), (), s32[]{:S(2)}) async-start(), calls=%async_computation.14 | async-start | bytes 1310720 | tf_op jit(solution)/shard_map/reduce_scatter | solution.py:54
  250.1 27.7 %copy-start.3 = (bf16[128,1024]{1,0:T(8,128)(2,1)S(1)}, bf16[128,1024]{1,0:T(8,128)(2,1)}, u32[]{:S(2)}) copy-start(bf16[128,1024]{1,0:T(8,128)(2,1)} %reduce-scatter.8.cloned.1.call-done) | copy-start | bytes 786436
  254.3 25.0 %copy-start.5 = (bf16[128,1024]{1,0:T(8,128)(2,1)S(1)}, bf16[128,1024]{1,0:T(8,128)(2,1)}, u32[]{:S(2)}) copy-start(bf16[128,1024]{1,0:T(8,128)(2,1)} %param.18) | copy-start | bytes 786436
  254.3 43.2 %all-gather.21.cloned.1.call-start = ((), (), s32[]{:S(2)}) async-start(), calls=%async_computation.15 | async-start | bytes 1310720 | tf_op jit(solution)/shard_map/all_gather | solution.py:50
  280.7 49.6 %reduce-scatter.12.cloned.1.call-start = ((), (), s32[]{:S(2)}) async-start(), calls=%async_computation.16 | async-start | bytes 1310720 | tf_op jit(solution)/shard_map/reduce_scatter | solution.py:54
  297.5 5.6 copy-start.19
  305.4 45.1 %all-gather.23.cloned.1.call-start = ((), (), s32[]{:S(2)}) async-start(), calls=%async_computation.17 | async-start | bytes 1310720 | tf_op jit(solution)/shard_map/all_gather | solution.py:50
  333.7 89.4 %reduce-scatter.18.cloned.1.call-start = ((), (), s32[]{:S(2)}) async-start(), calls=%async_computation.21 | async-start | bytes 2359296 | tf_op jit(solution)/shard_map/reduce_scatter | solution.py:185
  337.9 156.4 %reduce-scatter.20.cloned.1.call-start = ((), (), s32[]{:S(2)}) async-start(), calls=%async_computation.22 | async-start | bytes 2359296 | tf_op jit(solution)/shard_map/reduce_scatter | solution.py:182
  342.1 8.4 %copy-start.7 = (bf16[256,4,256]{0,2,1:T(8,128)(2,1)S(1)}, bf16[256,4,256]{0,2,1:T(8,128)(2,1)}, u32[]{:S(2)}) copy-start(bf16[256,4,256]{0,2,1:T(8,128)(2,1)} %copy-done.6) | copy-start | bytes 1572868
  342.2 13.6 %copy-start.16 = (bf16[4,128,4,64]{1,0,3,2:T(4,128)(2,1)S(1)}, bf16[4,128,4,64]{1,0,3,2:T(4,128)(2,1)}, u32[]{:S(2)}) copy-start(bf16[4,128,4,64]{1,0,3,2:T(4,128)(2,1)} %reshape.228) | copy-start | bytes 786436
  354.4 4.5 copy-start.15
  358.9 5.7 copy-start.11
  364.4 5.5 copy-start.12
  364.6 5.4 copy-start.13
  365.9 12.3 %all-to-all-start.1 = ((bf16[256,4,256]{2,0,1:T(8,128)(2,1)}), bf16[256,4,256]{2,0,1:T(8,128)(2,1)S(1)}, u32[]{:S(2)}, u32[]{:S(2)}) async-start(bf16[256,4,256]{2,0,1:T(8,128)(2,1)} %bitcast.152), calls=%async_computation.5 | async-start | bytes 1048576 | tf_op jit(solution)/shard_map/all_to_all | solution.py:191
  369.4 197.1 %reduce-scatter.16.cloned.1.call-start = ((), (), s32[]{:S(2)}) async-start(), calls=%async_computation.19 | async-start | bytes 2654208 | tf_op jit(solution)/shard_map/reduce_scatter | solution.py:225
  379.9 213.0 %reduce-scatter.14.cloned.1.call-start = ((), (), s32[]{:S(2)}) async-start(), calls=%async_computation.18 | async-start | bytes 1310720 | tf_op jit(solution)/shard_map/reduce_scatter | solution.py:54
  383.5 227.6 %all-gather.31.cloned.1.call-start = ((), (), s32[]{:S(2)}) async-start(), calls=%async_computation.25 | async-start | bytes 1310720 | tf_op jit(solution)/shard_map/all_gather | solution.py:230
  423.0 206.2 %all-gather.27.cloned.1.call-start = ((), (), s32[]{:S(2)}) async-start(), calls=%async_computation.23 | async-start | bytes 1310720 | tf_op jit(solution)/shard_map/all_gather | solution.py:50
  494.3 153.8 %all-gather.25.cloned.1.call-start = ((), (), s32[]{:S(2)}) async-start(), calls=%async_computation.20 | async-start | bytes 1474560 | tf_op jit(solution)/shard_map/all_gather | solution.py:232
  658.4 3.0 copy-start.1
  (8 other events, 10.6 us)
Sparse Core Ops, SparseCore 0:
  17.6 54.5 all-gather.28
  73.8 19.2 all-gather.12
  103.0 25.6 reduce-scatter.7
  131.2 50.3 all-gather.16
  183.5 14.8 all-gather.14
  201.0 49.0 all-gather.18
  254.5 23.2 reduce-scatter.9
  280.8 16.7 all-gather.20
  305.5 24.7 reduce-scatter.11
  333.8 16.6 all-gather.22
  354.6 68.3 reduce-scatter.17
  427.0 67.2 reduce-scatter.19
  497.8 68.6 reduce-scatter.15
  568.9 23.9 reduce-scatter.13
  594.3 16.6 all-gather.30
  612.5 16.6 all-gather.26
  630.6 17.4 all-gather.24

commit v2 on v1

--- a/solution.py
+++ b/solution.py
@@ -1,6 +1,8 @@
 import jax
 import jax.numpy as jnp
 from jax import lax
+from jax.experimental import pallas as pl
+from jax.experimental.pallas import tpu as pltpu
 from jax.sharding import PartitionSpec as P
 
 HEAD_DIM = 64
@@ -50,31 +52,263 @@
     return lax.all_gather(block, "rep", axis=0, tiled=True)
 
 
-def scatter_rep(partial):
-    return lax.psum_scatter(partial, "rep", scatter_dimension=0, tiled=True).astype(F32)
+MESH = pl.DeviceIdType.MESH
+CHUNK = 16
+
+
+class Peers:
+    def __init__(self, R):
+        self.R, self.A = R, R // 2
+        self.me = lax.axis_index("rep")
+        self.c = lax.rem(self.me, 2)
+        self.a = lax.div(self.me, 2)
+        self.partner = self.me + 1 - 2 * self.c
+
+    def chip(self, k):
+        return lax.rem(self.a + k, self.A)
+
+    def same(self, k):
+        return 2 * self.chip(k) + self.c
+
+    def other(self, k):
+        return 2 * self.chip(k) + 1 - self.c
+
+    def meet(self):
+        barrier = pltpu.get_barrier_semaphore()
+        for dev in [self.partner] + [self.same(k) for k in range(1, self.A)]:
+            pl.semaphore_signal(barrier, inc=1, device_id={"rep": dev}, device_id_type=MESH)
+        pl.semaphore_wait(barrier, self.A)
+
+
+def rows_of(index, T):
+    return pl.ds(pl.multiple_of(index * T, T), T)
+
+
+def chunk_rows(i, base=None):
+    start = i * CHUNK if base is None else base + i * CHUNK
+    return pl.ds(pl.multiple_of(start, CHUNK), CHUNK)
+
+
+def remote(src, dst, send, recv, dev):
+    return pltpu.make_async_remote_copy(
+        src_ref=src,
+        dst_ref=dst,
+        send_sem=send,
+        recv_sem=recv,
+        device_id={"rep": dev},
+        device_id_type=MESH,
+    )
+
+
+def scatter_sum(p, part, T, near, far, out, sems):
+    near_s, near_r, far_s, far_r = sems
+    order = list(range(1, p.A)) + [0]
+    first = {
+        k: remote(
+            part.at[rows_of(p.other(k), T)], near.at[k], near_s.at[k], near_r.at[k], p.partner
+        )
+        for k in order
+    }
+    for k in order:
+        first[k].start()
+    second = []
+    for k in range(1, p.A):
+        first[k].wait_recv()
+        base = p.same(k) * T
+
+        def add(i, _, k=k, base=base):
+            mine = part[chunk_rows(i, base), :].astype(F32)
+            out[k - 1, chunk_rows(i), :] = (mine + near[k, chunk_rows(i), :].astype(F32)).astype(BF)
+            return 0
+
+        lax.fori_loop(0, T // CHUNK, add, 0)
+        copy = remote(out.at[k - 1], far.at[k - 1], far_s.at[k - 1], far_r.at[k - 1], p.same(k))
+        copy.start()
+        second.append(copy)
+    first[0].wait_recv()
+    for copy in second:
+        copy.wait_recv()
+
+    def read(i):
+        total = part[chunk_rows(i, p.me * T), :].astype(F32) + near[0, chunk_rows(i), :].astype(F32)
+        for k in range(1, p.A):
+            total = total + far[k - 1, chunk_rows(i), :].astype(F32)
+        return total
+
+    return read, list(first.values()) + second
+
+
+def spread(p, src, full, T, sems):
+    dir_s, dir_r, fwd_s, fwd_r = sems
+    mine = full.at[rows_of(p.me, T)]
+    direct = {}
+    for k in list(range(1, p.A)) + [0]:
+        dev = p.partner if k == 0 else p.same(k)
+        direct[k] = remote(src, mine, dir_s.at[k], dir_r.at[k], dev)
+        direct[k].start()
+    passed = []
+    for k in range(1, p.A):
+        direct[k].wait_recv()
+        block = full.at[rows_of(p.same(p.A - k), T)]
+        copy = remote(block, block, fwd_s.at[k - 1], fwd_r.at[k - 1], p.partner)
+        copy.start()
+        passed.append(copy)
+    direct[0].wait_recv()
+    for copy in passed:
+        copy.wait_recv()
+    return list(direct.values()) + passed
+
+
+def drain(copies):
+    for copy in copies:
+        copy.wait_send()
+
+
+def run_kernel(kernel, cid, T, D, R, ins, outs, scatter, gather):
+    A = R // 2
+    few = max(A - 1, 1)
+    scratch = []
+    if scatter:
+        scratch += [
+            pltpu.VMEM((A, T, D), BF),
+            pltpu.VMEM((few, T, D), BF),
+            pltpu.VMEM((few, T, D), BF),
+        ]
+        scratch += [pltpu.SemaphoreType.DMA((n,)) for n in (A, A, few, few)]
+    if gather:
+        scratch += [pltpu.SemaphoreType.DMA((n,)) for n in (A, A, few, few)]
+    vmem = pl.BlockSpec(memory_space=pltpu.VMEM)
+    return pl.pallas_call(
+        kernel,
+        out_shape=[jax.ShapeDtypeStruct(*o) for o in outs],
+        in_specs=[vmem] * len(ins),
+        out_specs=[vmem] * len(outs),
+        scratch_shapes=scratch,
+        compiler_params=pltpu.CompilerParams(collective_id=cid, has_side_effects=True),
+        cost_estimate=pl.CostEstimate(flops=0, bytes_accessed=24 << 20, transcendentals=0),
+    )(*ins)
+
+
+def gather_kernel(block, R, cid):
+    T, D = block.shape
+
+    def kernel(src, full, *sems):
+        p = Peers(R)
+        p.meet()
+
+        def put(i, _):
+            full[chunk_rows(i, p.me * T), :] = src[chunk_rows(i), :]
+            return 0
+
+        lax.fori_loop(0, T // CHUNK, put, 0)
+        drain(spread(p, src, full, T, sems))
+
+    return run_kernel(kernel, cid, T, D, R, [block], [((R * T, D), BF)], False, True)[0]
 
 
 def norm_one_step(partial, x, bo, gone, sone):
-    resid = x.astype(F32) + scatter_rep(partial) + bo
-    normed, rstd = norm_parts(resid)
-    hidden = normed * gone + sone
-    return normed, rstd, hidden, gather_rep(hidden.astype(BF))
+    T, D = x.shape
+    R = partial.shape[0] // T
+
+    def kernel(part, xr, bor, gr, sr, normed_o, rstd_o, hidden_o, full, near, far, out, *sems):
+        p = Peers(R)
+        p.meet()
+        read, sent = scatter_sum(p, part, T, near, far, out, sems[:4])
+
+        def step(i, _):
+            normed, rstd = norm_parts(xr[chunk_rows(i), :].astype(F32) + read(i) + bor[...])
+            hidden = normed * gr[...] + sr[...]
+            normed_o[chunk_rows(i), :] = normed
+            rstd_o[chunk_rows(i), :] = rstd
+            hidden_o[chunk_rows(i), :] = hidden
+            full[chunk_rows(i, p.me * T), :] = hidden.astype(BF)
+            return 0
+
+        lax.fori_loop(0, T // CHUNK, step, 0)
+        drain(sent + spread(p, full.at[rows_of(p.me, T)], full, T, sems[4:]))
+
+    ins = [partial, x, bo[None], gone[None], sone[None]]
+    outs = [((T, D), F32), ((T, 1), F32), ((T, D), F32), ((R * T, D), BF)]
+    return run_kernel(kernel, 1, T, D, R, ins, outs, True, True)
+
+
+def add_sums(ref, values):
+    for n, v in enumerate(values):
+        ref[n : n + 1, :] += jnp.sum(v, axis=0, keepdims=True)
 
 
 def norm_two_step(partial, hidden, bd, gtwo, stwo, cot):
-    normed, rstd = norm_parts(hidden + scatter_rep(partial) + bd)
-    output = (normed * gtwo + stwo).astype(BF)
-    dout = cot.astype(F32)
-    d_two = norm_back(dout * gtwo, normed, rstd)
-    sums = (jnp.sum(d_two, 0), jnp.sum(dout * normed, 0), jnp.sum(dout, 0))
-    return output, d_two, sums, gather_rep(d_two.astype(BF))
+    T, D = hidden.shape
+    R = partial.shape[0] // T
+
+    def kernel(part, hr, br, gr, sr, cr, out_o, d_o, sums, full, near, far, out, *sems):
+        p = Peers(R)
+        p.meet()
+        sums[...] = jnp.zeros_like(sums)
+        read, sent = scatter_sum(p, part, T, near, far, out, sems[:4])
+
+        def step(i, _):
+            normed, rstd = norm_parts(hr[chunk_rows(i), :] + read(i) + br[...])
+            out_o[chunk_rows(i), :] = (normed * gr[...] + sr[...]).astype(BF)
+            dout = cr[chunk_rows(i), :].astype(F32)
+            d_two = norm_back(dout * gr[...], normed, rstd)
+            add_sums(sums, (d_two, dout * normed, dout))
+            d_o[chunk_rows(i), :] = d_two
+            full[chunk_rows(i, p.me * T), :] = d_two.astype(BF)
+            return 0
+
+        lax.fori_loop(0, T // CHUNK, step, 0)
+        drain(sent + spread(p, full.at[rows_of(p.me, T)], full, T, sems[4:]))
+
+    ins = [partial, hidden, bd[None], gtwo[None], stwo[None], cot]
+    outs = [((T, D), BF), ((T, D), F32), ((8, D), F32), ((R * T, D), BF)]
+    return run_kernel(kernel, 2, T, D, R, ins, outs, True, True)
 
 
 def back_one_step(partial, d_two, normed, rstd, gone):
-    d_hidden = d_two + scatter_rep(partial)
-    d_one = norm_back(d_hidden * gone, normed, rstd)
-    sums = (jnp.sum(d_one, 0), jnp.sum(d_hidden * normed, 0), jnp.sum(d_hidden, 0))
-    return d_one, sums, gather_rep(d_one.astype(BF))
+    T, D = d_two.shape
+    R = partial.shape[0] // T
+
+    def kernel(part, dr, nr, rr, gr, d_o, sums, full, near, far, out, *sems):
+        p = Peers(R)
+        p.meet()
+        sums[...] = jnp.zeros_like(sums)
+        read, sent = scatter_sum(p, part, T, near, far, out, sems[:4])
+
+        def step(i, _):
+            d_hidden = dr[chunk_rows(i), :] + read(i)
+            normed = nr[chunk_rows(i), :]
+            d_one = norm_back(d_hidden * gr[...], normed, rr[chunk_rows(i), :])
+            add_sums(sums, (d_one, d_hidden * normed, d_hidden))
+            d_o[chunk_rows(i), :] = d_one
+            full[chunk_rows(i, p.me * T), :] = d_one.astype(BF)
+            return 0
+
+        lax.fori_loop(0, T // CHUNK, step, 0)
+        drain(sent + spread(p, full.at[rows_of(p.me, T)], full, T, sems[4:]))
+
+    ins = [partial, d_two, normed, rstd, gone[None]]
+    outs = [((T, D), F32), ((8, D), F32), ((R * T, D), BF)]
+    return run_kernel(kernel, 3, T, D, R, ins, outs, True, True)
+
+
+def input_step(partial, d_one):
+    T, D = d_one.shape
+    R = partial.shape[0] // T
+
+    def kernel(part, dr, grad, near, far, out, *sems):
+        p = Peers(R)
+        p.meet()
+        read, sent = scatter_sum(p, part, T, near, far, out, sems)
+
+        def step(i, _):
+            grad[chunk_rows(i), :] = (dr[chunk_rows(i), :] + read(i)).astype(BF)
+            return 0
+
+        lax.fori_loop(0, T // CHUNK, step, 0)
+        drain(sent)
+
+    return run_kernel(kernel, 4, T, D, R, [partial, d_one], [((T, D), BF)], True, False)[0]
 
 
 def body(
@@ -132,7 +366,7 @@
         [jnp.concatenate([cols(w_query), cols(w_key), cols(w_value), cols(w_output)], 1), small], 0
     )
     got = lax.all_gather(pack, "shard", axis=0)
-    x_all = gather_rep(block_input)
+    x_all = gather_kernel(block_input, R, 0)
     wi_r = lax.dynamic_index_in_dim(w_inner.reshape(ds, S, R, fr), r, 2, keepdims=False)
     wi = lax.all_gather(wi_r.reshape(ds, S * fr), "shard", axis=0, tiled=True)
     wd = lax.all_gather(
@@ -224,7 +458,7 @@
     g_pack = jnp.concatenate([g_pack, g_small], 1)
     g_pack = lax.psum_scatter(g_pack, "shard", scatter_dimension=0, tiled=True)[0]
 
-    grad_input = (d_one + scatter_rep(in_part)).astype(BF)
+    grad_input = input_step(in_part, d_one)
 
     wd_out = gather_rep(g_wd).astype(F32)
     wi_out = lax.all_gather(g_wi, "rep", axis=0).astype(F32)

time: 669 us -> 499 us (0.75)
  waiting for transfers between devices: 530 us -> 283 us
  Pallas kernels: 0 us -> 97.8 us
  other arithmetic: 26.7 us -> 14.8 us
    pallas_call x0 -> x5, Pallas kernels: none -> 97.8 us  [run_kernel(): pl.pallas_call(kernel, out_shape=[jax.ShapeDtypeStruct(*o) for o in outs]...]
    reduce_scatter x4 -> x0, waiting for transfers between devices: 96.5 us -> none  [scatter_rep(): lax.psum_scatter(partial, 'rep', scatter_dimension=0, tiled=True)]
    all_gather x5 -> x1, waiting for transfers between devices: 67 us -> 11.4 us  [gather_rep(): return lax.all_gather(block, 'rep', axis=0, tiled=True)]
    all_gather x1, waiting for transfers between devices: 47.8 us -> 7.83 us  [body(): wi = lax.all_gather(wi_r.reshape(ds, S * fr), 'shard', axis=0, tiled=True)]
    reduce_scatter x1, waiting for transfers between devices: 39.4 us -> 1.65 us  [body(): lax.psum_scatter(mm_tn(hidden_all, d_inner_b).astype(BF), 'shard', scatte...]
    all_gather x1, waiting for transfers between devices: 53.9 us -> 39.2 us  [body(): got = lax.all_gather(pack, 'shard', axis=0)]
    all_gather x1, waiting for transfers between devices: 16.4 us -> 2.98 us  [body(): wi_out = lax.all_gather(g_wi, 'rep', axis=0).astype(F32)]
    all_to_all x1, waiting for transfers between devices: 0.01 us -> 7.45 us  [body(): lax.all_to_all(got[:, :ds, 3 * dr:].reshape(D, dr), 'rep', split_axis=0,...]
  transfers between devices with their start and end apart: 19 -> 11, of which waited for: 18 -> 11; matrix products, arithmetic and copies ran while one was open for 10% -> 11% of each run, Pallas kernels for 0% -> 15%
where the time goes in v2:
time: 499 us; the launch traced here: 498 us
  waiting for transfers between devices  283 us (57%)
  Pallas kernels  97.8 us (20%)
  matrix products  40.5 us (8%)
  local copies, waits for them, and re-layouts  39.4 us (8%)
  other arithmetic  14.8 us (3%)
  between operations  14.5 us (3%)
  starting transfers between devices  7.99 us (2%)
    pallas_call x5, Pallas kernels, run_kernel(): pl.pallas_call(kernel, out_shape=[jax.ShapeDtypeStruct(*o) for o in outs]...  97.8 us
    reduce_scatter x1, waiting for transfers between devices, body(): lax.psum_scatter(g_pack, 'shard', scatter_dimension=0, tiled=True)[0]  71.9 us
    reduce_scatter x1, waiting for transfers between devices, body(): lax.psum_scatter(mm_tn(acted, d_two_all).astype(BF), 'shard', scatter_dim...  71.2 us
    all_gather x1, waiting for transfers between devices, body(): lax.all_gather(lax.dynamic_slice(w_down, (r * fr, 0), (fr, D)), 'shard',...  45 us
    all_gather x1, waiting for transfers between devices, body(): got = lax.all_gather(pack, 'shard', axis=0)  39.2 us
    all_gather x1, waiting for transfers between devices, body(): packs = lax.all_gather(g_pack, 'rep', axis=0).astype(F32)  16.2 us
    unnamed x71, local copies, waits for them, and re-layouts  12.2 us
    dot_general x4, matrix products, mm_nt(): lax.dot_general(a, b, (((1,), (1,)), ((), ())), preferred_element_type=F32)  12 us
  transfers between devices with their start and end apart: 11, of which 11 were waited for; matrix products, arithmetic and copies ran while one was open for 11% of the time, Pallas kernels for 15%

profile of v2, /device:TPU:0, one launch (start us, length us, event | category | flops | bytes accessed | tf_op | source)
XLA Modules:
  0.0 497.8 jit_solution(14938745182882003308)
XLA Ops:
  19.9 13.2 %shard_map.296 = bf16[512,1024]{1,0:T(8,128)(2,1)} custom-call(bf16[128,1024]{1,0:T(8,128)(2,1)} %xr.1), custom_call_target="tpu_custom_call" | custom-call | bytes 25165824 | tf_op jit(solution)/shard_map/pallas_call | solution.py:181
  33.1 39.2 %all-gather.17.cloned.1.call-done = bf16[1152,1024]{1,0:T(8,128)(2,1)} async-done(((bf16[144,1024]{1,0:T(8,128)(2,1)}), bf16[1152,1024]{1,0:T(8,128)(2,1)}) %all-gather.17.cloned.1.call-update) | async-done | bytes 2359312 | tf_op jit(solution)/shard_map/all_gather | solution.py:368
  73.9 2.3 slice.171
  79.6 3.5 all-to-all-start
  84.4 7.4 %all-to-all-done = bf16[4,256,256]{2,1,0:T(8,128)(2,1)S(1)} async-done(((bf16[4,256,256]{2,1,0:T(8,128)(2,1)}), bf16[4,256,256]{2,1,0:T(8,128)(2,1)S(1)}, u32[]{:S(2)}, u32[]{:S(2)}) %all-to-all-start) | async-done | bytes 524320 | tf_op jit(solution)/shard_map/all_to_all | solution.py:376
  93.5 22.3 %shard_map.297 = (f32[128,1024]{1,0:T(8,128)}, f32[128,1]{1,0:T(8,128)}, f32[128,1024]{1,0:T(8,128)}, bf16[512,1024]{1,0:T(8,128)(2,1)}) custom-call(bf16[512,1024]{1,0:T(8,128)(2,1)} %convolution_convert_fusion.6.part, bf16[128,1024]{1,0:T(8,128)(2,1)} %xr.1, f32[1,1024]{1,0:T(1,128)} %bitcast.197, f32[1,1024]{1,0:T(1,128)} %bitcast.190, f32[1,1024]{1,0:T(1,128)} %bitcast.196), custom_call_target="tpu_custom_call" | custom-call | bytes 25165824 | tf_op jit(solution)/shard_map/pallas_call | solution.py:181
  115.9 7.8 %all-gather.9.cloned.1.call-done = bf16[1024,1024]{0,1:T(8,128)(2,1)} async-done(((bf16[128,1024]{0,1:T(8,128)(2,1)}), bf16[1024,1024]{0,1:T(8,128)(2,1)}) %all-gather.9.cloned.1.call-update) | async-done | bytes 2097168 | tf_op jit(solution)/shard_map/all_gather | solution.py:371
  123.7 5.0 %multiply_convert_fusion = (bf16[512,1024]{1,0:T(8,128)(2,1)}, f32[512,1024]{1,0:T(8,128)}) fusion(f32[1024]{0:T(1024)S(1)} %dynamic-slice_bitcast_fusion, bf16[512,1024]{1,0:T(8,128)(2,1)} %get-tuple-element.28, bf16[1024,1024]{0,1:T(8,128)(2,1)} %all-gather.9.cloned.1.call-done), kind=kOutput, calls=%fused_computation.10 | convolution fusion | flops 1076887552 | bytes 6295552 | tf_op jit(solution)/shard_map/dot_general | solution.py:36
  128.7 45.0 %all-gather.11.cloned.1.call-done = bf16[1024,1024]{1,0:T(8,128)(2,1)} async-done(((bf16[128,1024]{1,0:T(8,128)(2,1)}), bf16[1024,1024]{1,0:T(8,128)(2,1)}) %all-gather.11.cloned.1.call-update) | async-done | bytes 2097168 | tf_op jit(solution)/shard_map/all_gather | solution.py:372
  173.7 4.1 convolution_convert_fusion.5.part
  177.9 23.5 %shard_map.298 = (bf16[128,1024]{1,0:T(8,128)(2,1)}, f32[128,1024]{1,0:T(8,128)}, f32[8,1024]{1,0:T(8,128)}, bf16[512,1024]{1,0:T(8,128)(2,1)}) custom-call(bf16[512,1024]{1,0:T(8,128)(2,1)} %convolution_convert_fusion.5.part, f32[128,1024]{1,0:T(8,128)} %get-tuple-element.29.hr, f32[1,1024]{1,0:T(1,128)} %bitcast.195, f32[1,1024]{1,0:T(1,128)} %bitcast.194, ...), custom_call_target="tpu_custom_call" | custom-call | bytes 25165824 | tf_op jit(solution)/shard_map/pallas_call | solution.py:181
  201.4 4.5 fusion.53
  206.9 2.6 convolution_convert_fusion.1
  210.8 3.8 convolution_convert_fusion.4.part
  214.6 23.1 %shard_map.299 = (f32[128,1024]{1,0:T(8,128)}, f32[8,1024]{1,0:T(8,128)}, bf16[512,1024]{1,0:T(8,128)(2,1)}) custom-call(bf16[512,1024]{1,0:T(8,128)(2,1)} %convolution_convert_fusion.4.part, f32[128,1024]{1,0:T(8,128)} %get-tuple-element.32.dr, f32[128,1024]{1,0:T(8,128)} %get-tuple-element.33.nr, f32[128,1]{1,0:T(8,128)} %get-tuple-element.34.rr, ...), custom_call_target="tpu_custom_call" | custom-call | bytes 25165824 | tf_op jit(solution)/shard_map/pallas_call | solution.py:181
  241.1 4.2 convolution_convert_fusion
  249.4 2.8 fusion.47
  254.4 2.2 fusion.6
  256.6 1.7 copy.124
  260.8 3.5 all-to-all-start.1
  265.4 7.7 %all-to-all-done.1 = bf16[256,4,256]{2,0,1:T(8,128)(2,1)S(1)} async-done(((bf16[256,4,256]{2,0,1:T(8,128)(2,1)}), bf16[256,4,256]{2,0,1:T(8,128)(2,1)S(1)}, u32[]{:S(2)}, u32[]{:S(2)}) %all-to-all-start.1) | async-done | bytes 524320 | tf_op jit(solution)/shard_map/all_to_all | solution.py:425
  273.1 1.7 pad_maximum_fusion
  276.6 71.2 %reduce-scatter.8.cloned.1.call-done = bf16[128,1024]{1,0:T(8,128)(2,1)} async-done(((bf16[1024,1024]{1,0:T(8,128)(2,1)}), bf16[128,1024]{1,0:T(8,128)(2,1)}) %reduce-scatter.8.cloned.1.call-update) | async-done | bytes 262160 | tf_op jit(solution)/shard_map/reduce_scatter | solution.py:416
  348.2 71.9 %reduce-scatter.4.cloned.1.call-done = bf16[1,144,1024]{2,1,0:T(8,128)(2,1)} async-done(((bf16[8,144,1024]{2,1,0:T(8,128)(2,1)}), bf16[1,144,1024]{2,1,0:T(8,128)(2,1)}) %reduce-scatter.4.cloned.1.call-update) | async-done | bytes 294928 | tf_op jit(solution)/shard_map/reduce_scatter | solution.py:459
  420.2 2.0 convolution_convert_fusion.3.part
  422.2 15.6 %shard_map.300 = bf16[128,1024]{1,0:T(8,128)(2,1)} custom-call(bf16[512,1024]{1,0:T(8,128)(2,1)} %convolution_convert_fusion.3.part, f32[128,1024]{1,0:T(8,128)} %get-tuple-element.36.dr), custom_call_target="tpu_custom_call" | custom-call | bytes 25165824 | tf_op jit(solution)/shard_map/pallas_call | solution.py:181
  437.8 3.0 all-gather.19.cloned.1.call-done
  444.2 1.9 reshape.175
  446.1 11.4 %all-gather.15.cloned.1.call-done = bf16[512,1024]{1,0:T(8,128)(2,1)} async-done(((bf16[128,1024]{1,0:T(8,128)(2,1)}), bf16[512,1024]{1,0:T(8,128)(2,1)}) %all-gather.15.cloned.1.call-update) | async-done | bytes 1048592 | tf_op jit(solution)/shard_map/all_gather | solution.py:52
  457.5 2.8 convert_element_type.154
  460.3 16.2 %all-gather.13.cloned.1.call-done = bf16[4,144,1024]{2,1,0:T(8,128)(2,1)} async-done(((bf16[1,144,1024]{2,1,0:T(8,128)(2,1)}), bf16[4,144,1024]{2,1,0:T(8,128)(2,1)}) %all-gather.13.cloned.1.call-update) | async-done | bytes 1179664 | tf_op jit(solution)/shard_map/all_gather | solution.py:466
  480.6 2.2 reshape.168
  (164 shorter events, 53.7 us)
Async XLA Ops:
  7.2 11.9 %copy-start = (bf16[512,1024]{1,0:T(8,128)(2,1)S(1)}, bf16[512,1024]{1,0:T(8,128)(2,1)}, u32[]{:S(2)}) copy-start(bf16[512,1024]{1,0:T(8,128)(2,1)} %param.30) | copy-start | bytes 3145732
  7.2 10.4 %copy-start.9 = (bf16[128,4096]{1,0:T(8,128)(2,1)S(1)}, bf16[128,4096]{1,0:T(8,128)(2,1)}, u32[]{:S(2)}) copy-start(bf16[128,4096]{1,0:T(8,128)(2,1)} %param.28) | copy-start | bytes 3145732
  7.2 65.1 %all-gather.17.cloned.1.call-start = ((), (), s32[]{:S(2)}) async-start(), calls=%async_computation.12 | async-start | bytes 2654208 | tf_op jit(solution)/shard_map/all_gather | solution.py:368
  17.6 106.1 %all-gather.9.cloned.1.call-start = ((), (), s32[]{:S(2)}) async-start(), calls=%async_computation.5 | async-start | bytes 2359296 | tf_op jit(solution)/shard_map/all_gather | solution.py:371
  19.1 154.7 %all-gather.11.cloned.1.call-start = ((), (), s32[]{:S(2)}) async-start(), calls=%async_computation.6 | async-start | bytes 2359296 | tf_op jit(solution)/shard_map/all_gather | solution.py:372
  72.3 5.8 %copy-start.5 = (bf16[512,1024]{1,0:T(8,128)(2,1)S(1)}, bf16[512,1024]{1,0:T(8,128)(2,1)}, u32[]{:S(2)}) copy-start(bf16[512,1024]{1,0:T(8,128)(2,1)} %shard_map.296) | copy-start | bytes 3145732
  73.9 5.3 %copy-start.3 = (bf16[8,128,768]{2,1,0:T(8,128)(2,1)}, bf16[8,128,768]{2,1,0:T(8,128)(2,1)S(1)}, u32[]{:S(2)}) copy-start(bf16[8,128,768]{2,1,0:T(8,128)(2,1)S(1)} %slice.163) | copy-start | bytes 4718596
  79.4 4.4 copy-start.10
  79.6 12.3 %all-to-all-start = ((bf16[4,256,256]{2,1,0:T(8,128)(2,1)}), bf16[4,256,256]{2,1,0:T(8,128)(2,1)S(1)}, u32[]{:S(2)}, u32[]{:S(2)}) async-start(bf16[4,256,256]{2,1,0:T(8,128)(2,1)} %bitcast.6), calls=%async_computation | async-start | bytes 1048576 | tf_op jit(solution)/shard_map/all_to_all | solution.py:376
  83.1 193.5 %reduce-scatter.6.cloned.1.call-start = ((), (), s32[]{:S(2)}) async-start(), calls=%async_computation.9 | async-start | bytes 2359296 | tf_op jit(solution)/shard_map/reduce_scatter | solution.py:419
  201.4 5.5 %copy-start.17 = (bf16[512,1024]{1,0:T(8,128)(2,1)S(1)}, bf16[512,1024]{1,0:T(8,128)(2,1)}, u32[]{:S(2)}) copy-start(bf16[512,1024]{1,0:T(8,128)(2,1)} %get-tuple-element.28) | copy-start | bytes 3145732
  205.9 1.0 copy-start.18
  209.5 1.2 copy-start.19
  209.6 138.3 %reduce-scatter.8.cloned.1.call-start = ((), (), s32[]{:S(2)}) async-start(), calls=%async_computation.10 | async-start | bytes 2359296 | tf_op jit(solution)/shard_map/reduce_scatter | solution.py:416
  245.3 1.7 copy-start.11
  245.6 2.6 copy-start.8
  249.4 5.0 %copy-start.6 = (bf16[512,1024]{1,0:T(8,128)(2,1)S(1)}, bf16[512,1024]{1,0:T(8,128)(2,1)}, u32[]{:S(2)}) copy-start(bf16[512,1024]{1,0:T(8,128)(2,1)} %shard_map.296) | copy-start | bytes 3145732
  253.5 0.9 copy-start.13
  258.3 6.2 %copy-start.16 = (f32[8,1024]{1,0:T(8,128)S(1)}, f32[8,1024]{1,0:T(8,128)}, u32[]{:S(2)}) copy-start(f32[8,1024]{1,0:T(8,128)} %get-tuple-element.37) | copy-start | bytes 98308
  258.3 6.2 %copy-start.15 = (f32[8,1024]{1,0:T(8,128)S(1)}, f32[8,1024]{1,0:T(8,128)}, u32[]{:S(2)}) copy-start(f32[8,1024]{1,0:T(8,128)} %get-tuple-element.38) | copy-start | bytes 98308
  260.8 12.3 %all-to-all-start.1 = ((bf16[256,4,256]{2,0,1:T(8,128)(2,1)}), bf16[256,4,256]{2,0,1:T(8,128)(2,1)S(1)}, u32[]{:S(2)}, u32[]{:S(2)}) async-start(bf16[256,4,256]{2,0,1:T(8,128)(2,1)} %bitcast.146), calls=%async_computation.1 | async-start | bytes 1048576 | tf_op jit(solution)/shard_map/all_to_all | solution.py:425
  264.3 155.8 %reduce-scatter.4.cloned.1.call-start = ((), (), s32[]{:S(2)}) async-start(), calls=%async_computation.7 | async-start | bytes 2654208 | tf_op jit(solution)/shard_map/reduce_scatter | solution.py:459
  274.8 145.3 %copy-start.4 = (bf16[8,128,768]{2,1,0:T(8,128)(2,1)S(1)}, bf16[8,128,768]{2,1,0:T(8,128)(2,1)}, u32[]{:S(2)}) copy-start(bf16[8,128,768]{2,1,0:T(8,128)(2,1)} %copy-done.3) | copy-start | bytes 4718596
  274.9 145.3 %copy-start.14 = (bf16[512,768]{0,1:T(8,128)(2,1)S(1)}, bf16[512,768]{0,1:T(8,128)(2,1)}, u32[]{:S(2)}) copy-start(bf16[512,768]{0,1:T(8,128)(2,1)} %copy-done.13) | copy-start | bytes 2359300
  274.9 165.9 %all-gather.19.cloned.1.call-start = ((), (), s32[]{:S(2)}) async-start(), calls=%async_computation.13 | async-start | bytes 1310720 | tf_op jit(solution)/shard_map/all_gather | solution.py:464
  276.6 180.9 %all-gather.15.cloned.1.call-start = ((), (), s32[]{:S(2)}) async-start(), calls=%async_computation.11 | async-start | bytes 1310720 | tf_op jit(solution)/shard_map/all_gather | solution.py:52
  347.9 128.6 %all-gather.13.cloned.1.call-start = ((), (), s32[]{:S(2)}) async-start(), calls=%async_computation.8 | async-start | bytes 1474560 | tf_op jit(solution)/shard_map/all_gather | solution.py:466
  476.5 2.5 copy-start.2
  486.8 3.0 copy-start.12
  487.1 3.4 copy-start.7
  487.1 4.1 copy-start.1
Sparse Core Ops, SparseCore 0:
  17.7 54.5 all-gather.16
  74.9 48.7 all-gather.8
  126.4 47.2 all-gather.10
  209.7 66.8 reduce-scatter.5
  280.5 67.3 reduce-scatter.7
  351.2 68.8 reduce-scatter.3
  421.7 19.0 all-gather.18
  442.3 15.1 all-gather.14
  459.0 17.4 all-gather.12

commit v3 on v2

--- a/solution.py
+++ b/solution.py
@@ -46,10 +46,6 @@
 
 def ein(spec, a, b):
     return jnp.einsum(spec, a, b, preferred_element_type=F32)
-
-
-def gather_rep(block):
-    return lax.all_gather(block, "rep", axis=0, tiled=True)
 
 
 MESH = pl.DeviceIdType.MESH
@@ -368,10 +364,12 @@
     got = lax.all_gather(pack, "shard", axis=0)
     x_all = gather_kernel(block_input, R, 0)
     wi_r = lax.dynamic_index_in_dim(w_inner.reshape(ds, S, R, fr), r, 2, keepdims=False)
-    wi = lax.all_gather(wi_r.reshape(ds, S * fr), "shard", axis=0, tiled=True)
-    wd = lax.all_gather(
-        lax.dynamic_slice(w_down, (r * fr, 0), (fr, D)), "shard", axis=0, tiled=True
-    )
+    V = S * fr
+    dv = fr * D // V
+    wd_r = lax.dynamic_slice(w_down, (r * fr, 0), (fr, D)).reshape(dv, V)
+    mlp = lax.all_gather(jnp.concatenate([wi_r.reshape(ds, V), wd_r], 0), "shard", axis=0)
+    wi = mlp[:, :ds].reshape(D, V)
+    wd = mlp[:, ds:].reshape(V, D)
     wqkv = got[:, :ds, : 3 * dr].reshape(D, 3 * dr)
     wo = lax.all_to_all(
         got[:, :ds, 3 * dr :].reshape(D, dr), "rep", split_axis=0, concat_axis=1, tiled=True
@@ -413,12 +411,11 @@
     g_bias_inner = jnp.sum(d_inner, axis=0)
     d_inner_b = d_inner.astype(BF)
     hid_part = mm_nt(d_inner_b, wi).astype(BF)
-    g_wd = lax.psum_scatter(
-        mm_tn(acted, d_two_all).astype(BF), "shard", scatter_dimension=0, tiled=True
-    )
-    g_wi = lax.psum_scatter(
-        mm_tn(hidden_all, d_inner_b).astype(BF), "shard", scatter_dimension=0, tiled=True
-    )
+    g_wd = mm_tn(acted, d_two_all).astype(BF).reshape(S, dv, V)
+    g_wi = mm_tn(hidden_all, d_inner_b).astype(BF).reshape(S, ds, V)
+    g_mlp = lax.psum_scatter(
+        jnp.concatenate([g_wi, g_wd], 1), "shard", scatter_dimension=0, tiled=True
+    )[0]
 
     d_one, sums_one, d_one_all = back_one_step(hid_part, d_two, normed_one, rstd_one, gone)
     g_wo = mm_tn(context, d_one_all).astype(BF)
@@ -460,10 +457,10 @@
 
     grad_input = input_step(in_part, d_one)
 
-    wd_out = gather_rep(g_wd).astype(F32)
-    wi_out = lax.all_gather(g_wi, "rep", axis=0).astype(F32)
-    wi_out = wi_out.reshape(R, ds, S, fr).transpose(1, 2, 0, 3).reshape(ds, S * R * fr)
-    packs = lax.all_gather(g_pack, "rep", axis=0).astype(F32)
+    mlps = gather_kernel(g_mlp, R, 5).reshape(R, ds + dv, V).astype(F32)
+    wd_out = mlps[:, ds:].reshape(R * fr, D)
+    wi_out = mlps[:, :ds].reshape(R, ds, S, fr).transpose(1, 2, 0, 3).reshape(ds, S * R * fr)
+    packs = gather_kernel(g_pack, R, 6).reshape(R, ds + PAD, W).astype(F32)
     main = packs[:, :ds].reshape(R, ds, 4, dr).transpose(2, 1, 0, 3).reshape(4, ds, D)
     tail = packs[:, ds:].reshape(R, PAD * W)
     summed = jnp.sum(tail[:, : 8 * ds], axis=0)

time: 499 us -> 426 us (0.85)
  waiting for transfers between devices: 283 us -> 188 us
  Pallas kernels: 97.8 us -> 124 us
  matrix products: 40.5 us -> 30.7 us
  local copies, waits for them, and re-layouts: 39.4 us -> 46.7 us
    all_gather x5 -> x1, waiting for transfers between devices: 83.5 us -> 31.9 us  [body(): lax.all_gather(jnp.concatenate([wi_r.reshape(ds, V), wd_r], 0), 'shard',...]
    reduce_scatter x1, waiting for transfers between devices: 71.9 us -> 45.2 us  [body(): lax.psum_scatter(g_pack, 'shard', scatter_dimension=0, tiled=True)[0]]
    pallas_call x5 -> x7, Pallas kernels: 97.8 us -> 124 us  [run_kernel(): pl.pallas_call(kernel, out_shape=[jax.ShapeDtypeStruct(*o) for o in outs]...]
    reduce_scatter x2 -> x1, waiting for transfers between devices: 72.9 us -> 64.1 us  [body(): lax.psum_scatter(jnp.concatenate([g_wi, g_wd], 1), 'shard', scatter_dimen...]
    unnamed x71 -> x81, local copies, waits for them, and re-layouts: 12.2 us -> 14.9 us
  transfers between devices with their start and end apart: 11 -> 6, of which waited for: 11 -> 6; matrix products, arithmetic and copies ran while one was open for 11% -> 10% of each run, Pallas kernels for 15% -> 14%
where the time goes in v3:
time: 426 us; the launch traced here: 425 us
  waiting for transfers between devices  188 us (44%)
  Pallas kernels  124 us (29%)
  local copies, waits for them, and re-layouts  46.7 us (11%)
  matrix products  30.7 us (7%)
  between operations  14.5 us (3%)
  other arithmetic  13.8 us (3%)
  starting transfers between devices  7.31 us (2%)
    pallas_call x7, Pallas kernels, run_kernel(): pl.pallas_call(kernel, out_shape=[jax.ShapeDtypeStruct(*o) for o in outs]...  124 us
    reduce_scatter x1, waiting for transfers between devices, body(): lax.psum_scatter(jnp.concatenate([g_wi, g_wd], 1), 'shard', scatter_dimen...  64.1 us
    reduce_scatter x1, waiting for transfers between devices, body(): lax.psum_scatter(g_pack, 'shard', scatter_dimension=0, tiled=True)[0]  45.2 us
    all_gather x1, waiting for transfers between devices, body(): got = lax.all_gather(pack, 'shard', axis=0)  38.2 us
    all_gather x1, waiting for transfers between devices, body(): lax.all_gather(jnp.concatenate([wi_r.reshape(ds, V), wd_r], 0), 'shard',...  31.9 us
    unnamed x81, local copies, waits for them, and re-layouts  14.9 us
    dot_general x4, matrix products, mm_nt(): lax.dot_general(a, b, (((1,), (1,)), ((), ())), preferred_element_type=F32)  10.5 us
    dot_general x4, matrix products, mm(): return jnp.dot(a, b, preferred_element_type=F32)  8.83 us
  transfers between devices with their start and end apart: 6, of which 6 were waited for; matrix products, arithmetic and copies ran while one was open for 10% of the time, Pallas kernels for 14%

profile of v3, /device:TPU:0, one launch (start us, length us, event | category | flops | bytes accessed | tf_op | source)
XLA Modules:
  0.0 424.8 jit_solution(1629359291984794841)
XLA Ops:
  20.9 13.2 %shard_map.296 = bf16[512,1024]{1,0:T(8,128)(2,1)} custom-call(bf16[128,1024]{1,0:T(8,128)(2,1)} %xr.1), custom_call_target="tpu_custom_call" | custom-call | bytes 25165824 | tf_op jit(solution)/shard_map/pallas_call | solution.py:177
  34.1 38.2 %all-gather.5.cloned.1.call-done = bf16[1152,1024]{1,0:T(8,128)(2,1)} async-done(((bf16[144,1024]{1,0:T(8,128)(2,1)}), bf16[1152,1024]{1,0:T(8,128)(2,1)}) %all-gather.5.cloned.1.call-update) | async-done | bytes 2359312 | tf_op jit(solution)/shard_map/all_gather | solution.py:364
  72.3 1.9 slice.187
  74.2 2.8 slice.179
  78.0 3.7 all-to-all-start
  82.5 2.4 convolution_bitcast_fusion
  86.5 3.9 all-to-all-done
  92.0 22.4 %shard_map.297 = (f32[128,1024]{1,0:T(8,128)}, f32[128,1]{1,0:T(8,128)}, f32[128,1024]{1,0:T(8,128)}, bf16[512,1024]{1,0:T(8,128)(2,1)}) custom-call(bf16[512,1024]{1,0:T(8,128)(2,1)} %convolution_convert_fusion.6.part, bf16[128,1024]{1,0:T(8,128)(2,1)} %xr.1, f32[1,1024]{1,0:T(1,128)} %bitcast.227, f32[1,1024]{1,0:T(1,128)} %bitcast.220, f32[1,1024]{1,0:T(1,128)} %bitcast.226), custom_call_target="tpu_custom_call" | custom-call | bytes 25165824 | tf_op jit(solution)/shard_map/pallas_call | solution.py:177
  114.4 31.9 %all-gather.7.cloned.1.call-done = bf16[2048,1024]{1,0:T(8,128)(2,1)} async-done(((bf16[256,1024]{1,0:T(8,128)(2,1)}), bf16[2048,1024]{1,0:T(8,128)(2,1)}) %all-gather.7.cloned.1.call-update) | async-done | bytes 4194320 | tf_op jit(solution)/shard_map/all_gather | solution.py:370
  146.4 2.8 fusion.45
  149.2 2.7 multiply_convert_fusion
  151.9 2.2 convolution_convert_fusion.5.part
  154.2 23.5 %shard_map.298 = (bf16[128,1024]{1,0:T(8,128)(2,1)}, f32[128,1024]{1,0:T(8,128)}, f32[8,1024]{1,0:T(8,128)}, bf16[512,1024]{1,0:T(8,128)(2,1)}) custom-call(bf16[512,1024]{1,0:T(8,128)(2,1)} %convolution_convert_fusion.5.part, f32[128,1024]{1,0:T(8,128)} %get-tuple-element.29.hr, f32[1,1024]{1,0:T(1,128)} %bitcast.225, f32[1,1024]{1,0:T(1,128)} %bitcast.224, ...), custom_call_target="tpu_custom_call" | custom-call | bytes 25165824 | tf_op jit(solution)/shard_map/pallas_call | solution.py:177
  177.7 4.6 %fusion.55 = (bf16[1024]{0:T(1024)(128)(2,1)S(1)}, bf16[512,1024]{1,0:T(8,128)(2,1)S(1)}) fusion(f32[512,1024]{1,0:T(8,128)} %get-tuple-element.78, f32[1024]{0:T(1024)S(1)} %dynamic-slice_bitcast_fusion, bf16[512,1024]{1,0:T(8,128)(2,1)} %get-tuple-element.31, bf16[1024,1024]{1,0:T(8,128)(2,1)} %bitcast.190), kind=kOutput, calls=%fused_computation.115 | convolution fusion | flops 1080032256 | bytes 6297600 | tf_op jit(solution)/shard_map/dot_general | solution.py:40
  182.3 2.3 convolution_convert_fusion.4.part
  184.5 23.2 %shard_map.299 = (f32[128,1024]{1,0:T(8,128)}, f32[8,1024]{1,0:T(8,128)}, bf16[512,1024]{1,0:T(8,128)(2,1)}) custom-call(bf16[512,1024]{1,0:T(8,128)(2,1)} %convolution_convert_fusion.4.part, f32[128,1024]{1,0:T(8,128)} %get-tuple-element.32.dr, f32[128,1024]{1,0:T(8,128)} %get-tuple-element.33.nr, f32[128,1]{1,0:T(8,128)} %get-tuple-element.34.rr, ...), custom_call_target="tpu_custom_call" | custom-call | bytes 25165824 | tf_op jit(solution)/shard_map/pallas_call | solution.py:177
  212.5 2.2 fusion.12
  218.4 3.5 all-to-all-start.1
  222.5 2.1 fusion.6
  226.4 4.3 %all-to-all-done.1 = bf16[256,4,256]{2,0,1:T(8,128)(2,1)S(1)} async-done(((bf16[256,4,256]{2,0,1:T(8,128)(2,1)}), bf16[256,4,256]{2,0,1:T(8,128)(2,1)S(1)}, u32[]{:S(2)}, u32[]{:S(2)}) %all-to-all-start.1) | async-done | bytes 524320 | tf_op jit(solution)/shard_map/all_to_all | solution.py:422
  233.6 2.6 convolution_convert_fusion
  237.5 2.4 pad_maximum_fusion
  241.3 2.0 convolution_convert_fusion.3.part
  243.3 11.3 %shard_map.300 = bf16[128,1024]{1,0:T(8,128)(2,1)} custom-call(bf16[512,1024]{1,0:T(8,128)(2,1)} %convolution_convert_fusion.3.part, f32[128,1024]{1,0:T(8,128)} %get-tuple-element.36.dr), custom_call_target="tpu_custom_call" | custom-call | bytes 25165824 | tf_op jit(solution)/shard_map/pallas_call | solution.py:177
  254.6 45.2 %reduce-scatter.3.cloned.1.call-done = bf16[1,144,1024]{2,1,0:T(8,128)(2,1)} async-done(((bf16[8,144,1024]{2,1,0:T(8,128)(2,1)}), bf16[1,144,1024]{2,1,0:T(8,128)(2,1)}) %reduce-scatter.3.cloned.1.call-update) | async-done | bytes 294928 | tf_op jit(solution)/shard_map/reduce_scatter | solution.py:456
  299.9 12.4 %shard_map.301 = bf16[576,1024]{1,0:T(8,128)(2,1)} custom-call(bf16[144,1024]{1,0:T(8,128)(2,1)} %bitcast.214), custom_call_target="tpu_custom_call" | custom-call | bytes 25165824 | tf_op jit(solution)/shard_map/pallas_call | solution.py:177
  315.6 2.0 reshape.187
  317.5 3.0 copy.152
  326.7 64.1 %reduce-scatter.5.cloned.1.call-done = bf16[1,256,1024]{2,1,0:T(8,128)(2,1)} async-done(((bf16[8,256,1024]{2,1,0:T(8,128)(2,1)}), bf16[1,256,1024]{2,1,0:T(8,128)(2,1)}) %reduce-scatter.5.cloned.1.call-update) | async-done | bytes 524304 | tf_op jit(solution)/shard_map/reduce_scatter | solution.py:416
  390.9 18.1 %shard_map.302 = bf16[1024,1024]{1,0:T(8,128)(2,1)} custom-call(bf16[256,1024]{1,0:T(8,128)(2,1)} %bitcast.206), custom_call_target="tpu_custom_call" | custom-call | bytes 25165824 | tf_op jit(solution)/shard_map/pallas_call | solution.py:177
  409.0 3.2 fusion.46
  414.0 1.9 reshape.192
  (160 shorter events, 48.5 us)
Async XLA Ops:
  7.2 12.8 %copy-start = (bf16[512,1024]{1,0:T(8,128)(2,1)S(1)}, bf16[512,1024]{1,0:T(8,128)(2,1)}, u32[]{:S(2)}) copy-start(bf16[512,1024]{1,0:T(8,128)(2,1)} %param.30) | copy-start | bytes 3145732
  7.2 10.4 %copy-start.12 = (bf16[128,4096]{1,0:T(8,128)(2,1)S(1)}, bf16[128,4096]{1,0:T(8,128)(2,1)}, u32[]{:S(2)}) copy-start(bf16[128,4096]{1,0:T(8,128)(2,1)} %param.28) | copy-start | bytes 3145732
  7.2 65.1 %all-gather.5.cloned.1.call-start = ((), (), s32[]{:S(2)}) async-start(), calls=%async_computation.6 | async-start | bytes 2654208 | tf_op jit(solution)/shard_map/all_gather | solution.py:364
  17.6 128.8 %all-gather.7.cloned.1.call-start = ((), (), s32[]{:S(2)}) async-start(), calls=%async_computation.7 | async-start | bytes 4718592 | tf_op jit(solution)/shard_map/all_gather | solution.py:370
  74.2 8.4 %copy-start.7 = (bf16[512,1024]{1,0:T(8,128)(2,1)S(1)}, bf16[512,1024]{1,0:T(8,128)(2,1)}, u32[]{:S(2)}) copy-start(bf16[512,1024]{1,0:T(8,128)(2,1)} %shard_map.296) | copy-start | bytes 3145732
  78.0 12.3 %all-to-all-start = ((bf16[4,256,256]{2,1,0:T(8,128)(2,1)}), bf16[4,256,256]{2,1,0:T(8,128)(2,1)S(1)}, u32[]{:S(2)}, u32[]{:S(2)}) async-start(bf16[4,256,256]{2,1,0:T(8,128)(2,1)} %bitcast.6), calls=%async_computation | async-start | bytes 1048576 | tf_op jit(solution)/shard_map/all_to_all | solution.py:374
  85.3 0.9 copy-start.13
  146.4 2.8 copy-start.19
  149.2 2.7 copy-start.3
  149.2 2.7 copy-start.5
  151.9 2.2 copy-start.22
  177.7 4.6 %copy-start.4 = (bf16[8,128,1024]{2,1,0:T(8,128)(2,1)S(1)}, bf16[8,128,1024]{2,1,0:T(8,128)(2,1)}, u32[]{:S(2)}) copy-start(bf16[8,128,1024]{2,1,0:T(8,128)(2,1)} %copy-done.3) | copy-start | bytes 6291460
  182.3 2.3 copy-start.23
  209.7 2.8 copy-start.14
  210.3 1.0 copy-start.11
  212.5 2.7 copy-start.9
  214.6 1.1 copy-start.15
  215.2 2.2 copy-start.18
  215.2 2.3 copy-start.17
  216.8 5.1 %copy-start.16 = (bf16[512,768]{0,1:T(8,128)(2,1)S(1)}, bf16[512,768]{0,1:T(8,128)(2,1)}, u32[]{:S(2)}) copy-start(bf16[512,768]{0,1:T(8,128)(2,1)} %bitcast_dynamic-update-slice_fusion.2) | copy-start | bytes 2359300
  217.1 5.4 %copy-start.8 = (bf16[512,1024]{1,0:T(8,128)(2,1)S(1)}, bf16[512,1024]{1,0:T(8,128)(2,1)}, u32[]{:S(2)}) copy-start(bf16[512,1024]{1,0:T(8,128)(2,1)} %shard_map.296) | copy-start | bytes 3145732
  218.4 12.3 %all-to-all-start.1 = ((bf16[256,4,256]{2,0,1:T(8,128)(2,1)}), bf16[256,4,256]{2,0,1:T(8,128)(2,1)S(1)}, u32[]{:S(2)}, u32[]{:S(2)}) async-start(bf16[256,4,256]{2,0,1:T(8,128)(2,1)} %bitcast.161), calls=%async_computation.1 | async-start | bytes 1048576 | tf_op jit(solution)/shard_map/all_to_all | solution.py:422
  221.9 78.0 %reduce-scatter.3.cloned.1.call-start = ((), (), s32[]{:S(2)}) async-start(), calls=%async_computation.4 | async-start | bytes 2654208 | tf_op jit(solution)/shard_map/reduce_scatter | solution.py:456
  232.4 1.2 copy-start.21
  232.4 3.8 copy-start.20
  232.4 158.4 %reduce-scatter.5.cloned.1.call-start = ((), (), s32[]{:S(2)}) async-start(), calls=%async_computation.5 | async-start | bytes 4718592 | tf_op jit(solution)/shard_map/reduce_scatter | solution.py:416
  233.6 2.6 copy-start.24
  239.9 1.4 copy-start.6
  312.3 1.6 copy-start.2
  414.0 4.3 %copy-start.1 = (bf16[512,1024]{1,0:T(8,128)(2,1)S(1)}, bf16[512,1024]{1,0:T(8,128)(2,1)}, u32[]{:S(2)}) copy-start(bf16[512,1024]{1,0:T(8,128)(2,1)} %param.30) | copy-start | bytes 3145732
  414.0 3.5 copy-start.10
Sparse Core Ops, SparseCore 0:
  17.7 54.5 all-gather.4
  75.0 71.3 all-gather.6
  232.5 67.3 reduce-scatter.2
  303.3 87.4 reduce-scatter.4
